TPU v7x, 32 devices: a whole 2x2x4 slice. The times are simulated.
32 devices in a mesh: items: 8 (over z, y), narrow: 4 (over x, core).
Axes of the slice: x: 2, y: 2, z: 4, core: 2. Of those that a mesh axis runs over, the one named last changes fastest.
Arguments:
- tokens: bfloat16 [32, 512, 768], P('items', 'narrow'), may hold values from -6 to 6
- memory: bfloat16 [32, 2048, 768], P('items', 'narrow'), may hold values from -6 to 6
- mem_count: int32 [32], P('items'), may hold values from 768 to 2048, as said below
- cotangent: bfloat16 [32, 512, 768], P('items', 'narrow'), may hold values from -6 to 6
- gain_self: float32 [768], replicated, may hold values from 0.1 to 1.9
- self_query: bfloat16 [768, 768], replicated, may hold values from -0.0546875 to 0.0546875
- self_key: bfloat16 [768, 768], replicated, may hold values from -0.21875 to 0.21875
- self_value: bfloat16 [768, 768], replicated, may hold values from -0.21875 to 0.21875
- self_out: bfloat16 [768, 768], replicated, may hold values from -0.625 to 0.625
- gain_cross: float32 [768], replicated, may hold values from 0.1 to 1.9
- cross_query: bfloat16 [768, 768], replicated, may hold values from -0.0546875 to 0.0546875
- cross_key: bfloat16 [768, 768], replicated, may hold values from -0.21875 to 0.21875
- cross_value: bfloat16 [768, 768], replicated, may hold values from -0.21875 to 0.21875
- cross_out: bfloat16 [768, 768], replicated, may hold values from -1.25 to 1.25
- gain_feed: float32 [768], replicated, may hold values from 0.1 to 1.9
- gate_weight: bfloat16 [768, 2048], replicated, may hold values from -0.21875 to 0.21875
- up_weight: bfloat16 [768, 2048], replicated, may hold values from -0.21875 to 0.21875
- down_weight: bfloat16 [2048, 768], replicated, may hold values from -0.1875 to 0.1875
Outputs:
- result: bfloat16 [32, 512, 768], P('items', 'narrow')
- tokens_grad: float32 [32, 512, 768], P('items', 'narrow')
- memory_grad: float32 [32, 2048, 768], P('items', 'narrow')
- gain_self_grad: float32 [768], replicated
- self_query_grad: float32 [768, 768], P('items', 'narrow')
- self_key_grad: float32 [768, 768], P('items', 'narrow')
- self_value_grad: float32 [768, 768], P('items', 'narrow')
- self_out_grad: float32 [768, 768], P('items', 'narrow')
- gain_cross_grad: float32 [768], replicated
- cross_query_grad: float32 [768, 768], P('items', 'narrow')
- cross_key_grad: float32 [768, 768], P('items', 'narrow')
- cross_value_grad: float32 [768, 768], P('items', 'narrow')
- cross_out_grad: float32 [768, 768], P('items', 'narrow')
- gain_feed_grad: float32 [768], replicated
- gate_weight_grad: float32 [768, 2048], P('items', 'narrow')
- up_weight_grad: float32 [768, 2048], P('items', 'narrow')
- down_weight_grad: float32 [2048, 768], P('items', 'narrow')
Inputs may be any that keep to these rules, and one draw needn't show every extreme that they name: `mem_count`: each item's count is 2048, 1024 or 768; memory rows at and past the count are padding, and every draw has items with 2048 and with 768 patches.
All inputs are finite; a program needn't handle non-finite values.
Results may differ from a plain program's by a relative error of at most 0.02555.
The roundings to bfloat16 on the way count: a program that leaves them out, or rounds other values in their place, can miss the bound.
Values may be sent and summed in bfloat16 or wider, within the bound.
No kernel may reach another device: no remote copies, remote signals or barrier semaphores. Data moves between devices by JAX's collectives and lax.ppermute only.
A program may use at most 320 MiB of HBM per device.

v0:
```python
import jax
import jax.numpy as jnp
from jax import lax
from jax.experimental import pallas as pl
from jax.experimental.pallas import tpu as pltpu
from jax.sharding import PartitionSpec as P

HD = 64
LANES = 128
BLOCKS = 8

eps = 1e-06
neg_big = -1e30
smallest_total = 1e-25
gelu_scale = 0.7978845608028654
gelu_cubic = 0.044715
low = jnp.bfloat16
high = jnp.float32
vmem_bytes = 60 * 1024 * 1024


def rows_dot(left_side, right_side):
    return lax.dot_general(
        left_side, right_side, (((1,), (1,)), ((), ())), preferred_element_type=high
    )


def cols_dot(left_side, right_side):
    return lax.dot_general(
        left_side, right_side, (((0,), (0,)), ((), ())), preferred_element_type=high
    )


def plain_dot(left_side, right_side):
    return jnp.dot(left_side, right_side, preferred_element_type=high)


def inverse_scale(hidden):
    return lax.rsqrt(jnp.mean(hidden * hidden, axis=-1, keepdims=True) + eps)


def norm_back(hidden, gain, grad):
    scale = inverse_scale(hidden)
    weighted = gain * grad
    middle = jnp.mean(weighted * hidden, axis=-1, keepdims=True)
    to_rows = scale * (weighted - hidden * (scale * scale * middle))
    to_gain = jnp.sum(grad * hidden * scale, axis=0, keepdims=True)
    return to_rows, to_gain


call_time = {
    "enter_memory_near": 2,
    "self_forward": 8,
    "cross_forward_near": 6,
    "enter_memory_far": 2,
    "cross_forward_far": 6,
    "cross_backward_far_b": 100,
    "feed_weights_two": 100,
    "memory_back": 100,
    "self_weights_two": 100,
    "self_weights_end": 100,
}


def cost(name):
    return pl.CostEstimate(
        flops=int(call_time.get(name, 0.001) * 1.15e9), bytes_accessed=1, transcendentals=0
    )


def after(piece, *earlier):
    return lax.optimization_barrier((piece, *earlier))[0]


def row_spec(rows, width):
    return pl.BlockSpec((rows, width), lambda step: (step, 0))


def whole_spec(shape):
    return pl.BlockSpec(
        shape, lambda step: (0,) * len(shape), pipeline_mode=pl.Buffered(1)
    )


def self_forward(
    tokens_ref,
    gains_ref,
    next_query_ref,
    wq_ref,
    wk_ref,
    wv_ref,
    out_ref,
    normed_ref,
    q_ref,
    k_ref,
    v_ref,
    weight_ref,
    mixed_ref,
    inverse_ref,
    hidden_ref,
    next_normed_ref,
    next_q_ref,
    stats_ref,
    part_ref,
):
    pair = pl.program_id(0)

    @pl.when(pair == 0)
    def _():
        hidden = tokens_ref[...].astype(high)
        normed_ref[...] = (hidden * inverse_scale(hidden) * gains_ref[0:1, :]).astype(low)
        hidden_ref[...] = hidden

    weights = jnp.concatenate([wq_ref[...], wk_ref[...], wv_ref[...]], axis=1)
    projected = plain_dot(normed_ref[...], weights).astype(low)
    for at, head_ref in enumerate((q_ref, k_ref, v_ref)):
        head_ref[...] = projected[:, at * LANES : (at + 1) * LANES]
    attend_forward_kernel(
        True,
        1,
        0,
        True,
        None,
        q_ref,
        k_ref,
        v_ref,
        weight_ref,
        mixed_ref,
        inverse_ref,
        stats_ref,
        part_ref,
    )
    hidden_ref[...] += plain_dot(mixed_ref[...], out_ref[...])

    @pl.when(pair == pl.num_programs(0) - 1)
    def _():
        hidden = hidden_ref[...]
        normed = (hidden * inverse_scale(hidden) * gains_ref[1:2, :]).astype(low)
        next_normed_ref[...] = normed
        next_q_ref[...] = plain_dot(normed, next_query_ref[...]).astype(low)


def self_forward_call(tokens, gains, next_query, wq, wk, wv, out_weight):
    rows, width = tokens.shape
    pairs = width // LANES
    whole = pl.BlockSpec((rows, width), lambda pair: (0, 0))
    columns = pl.BlockSpec((rows, LANES), lambda pair: (0, pair))
    stack = lambda height: pl.BlockSpec((1, height, 2 * rows), lambda pair: (pair, 0, 0))
    plain = jax.ShapeDtypeStruct((rows, width), low)
    return pl.pallas_call(
        self_forward,
        grid=(pairs,),
        in_specs=[whole_spec(piece.shape) for piece in (tokens, gains, next_query)]
        + [pl.BlockSpec((width, LANES), lambda pair: (0, pair))] * 3
        + [pl.BlockSpec((LANES, width), lambda pair: (pair, 0))],
        out_specs=[whole, columns, columns, columns, stack(rows), columns, stack(8)] + [whole] * 3,
        out_shape=[
            plain,
            plain,
            plain,
            plain,
            jax.ShapeDtypeStruct((pairs, rows, 2 * rows), low),
            plain,
            jax.ShapeDtypeStruct((pairs, 8, 2 * rows), high),
            jax.ShapeDtypeStruct((rows, width), high),
            plain,
            plain,
        ],
        scratch_shapes=[
            pltpu.VMEM((2, 2 * rows), high),
            pltpu.VMEM((1, LANES, 2 * rows), high),
        ],
        cost_estimate=cost("self_forward"),
        compiler_params=pltpu.CompilerParams(vmem_limit_bytes=vmem_bytes),
        name="self_forward",
    )(tokens, gains, next_query, wq, wk, wv, out_weight)


def enter_memory(first_ref, second_ref, wk_ref, wv_ref, rows_ref, k_ref, v_ref):
    half = first_ref.shape[0]
    for at, piece_ref in ((0, first_ref), (half, second_ref)):
        rows = piece_ref[...]
        rows_ref[at : at + half, :] = rows
        k_ref[at : at + half, :] = plain_dot(rows, wk_ref[...]).astype(low)
        v_ref[at : at + half, :] = plain_dot(rows, wv_ref[...]).astype(low)


def one_step_call(kernel, name, ins, outs, scratch=()):
    vmem = pl.BlockSpec(memory_space=pltpu.VMEM)
    smem = pl.BlockSpec(memory_space=pltpu.SMEM)
    return pl.pallas_call(
        kernel,
        in_specs=[smem if piece.dtype == jnp.int32 else vmem for piece in ins],
        out_specs=[vmem] * len(outs),
        out_shape=[jax.ShapeDtypeStruct(shape, kind) for shape, kind in outs],
        scratch_shapes=list(scratch),
        cost_estimate=cost(name),
        compiler_params=pltpu.CompilerParams(vmem_limit_bytes=vmem_bytes),
        name=name,
    )(*ins)


def put_block(parcel, job, tile, rows_of, out_ref, spot):
    plain, rows = parcel.plain[job], parcel.heights[job]
    if tile < 2 * plain:
        at = (tile // plain) * parcel.own + parcel.at[job] + (tile % plain) * rows
        out_ref[spot, at : at + rows, :] = rows_of
    else:
        half = LANES // 2
        for side in (0, 1):
            at = side * parcel.own + parcel.at[job] + plain * rows
            lanes = slice(side * half, (side + 1) * half)
            out_ref[spot, at : at + rows // 2, :] = jnp.concatenate(
                [rows_of[: rows // 2, lanes], rows_of[rows // 2 :, lanes]], axis=1
            )


def put_rows(parcel, job, product, tile, out_ref, slot):
    rows = parcel.heights[job]
    for block in range(BLOCKS):
        put_block(
            parcel,
            job,
            tile,
            product[block * rows : (block + 1) * rows, slot * LANES : (slot + 1) * LANES],
            out_ref,
            place(block),
        )


def feed_both(
    parcel,
    parts,
    core_ref,
    crossed_ref,
    hidden_in_ref,
    cotangent_ref,
    gain_ref,
    out_ref,
    gate_ref,
    up_ref,
    down_ref,
    result_ref,
    grad_hidden_ref,
    branch_ref,
    grad_crossed_ref,
    grad_gain_ref,
    kept_out_ref,
    sent_out_ref,
    hidden_ref,
    normed_ref,
    turned_ref,
    sum_ref,
    back_ref,
    sides_ref,
    kept_ref,
    sent_ref,
    done_ref,
):
    step = pl.program_id(0)
    core = core_ref[0]
    gain = gain_ref[2:3, :]

    @pl.when(step == 0)
    def _():
        hidden = hidden_in_ref[...] + plain_dot(crossed_ref[...], out_ref[...])
        hidden_ref[...] = hidden
        normed = (hidden * inverse_scale(hidden) * gain).astype(low)
        normed_ref[...] = normed
        turned_ref[...] = normed.T
        sum_ref[...] = hidden
        back_ref[...] = jnp.zeros_like(back_ref)
        sides_ref[...] = jnp.concatenate(both_sides(cotangent_ref[...], core), axis=1)

    inner = parcel.at[2]

    def copies(side_ref, out_ref, begin, rows, slot):
        here = (slice(None), pl.ds(begin, rows), slice(None))
        return pltpu.make_async_copy(side_ref.at[here], out_ref.at[here], done_ref.at[slot])

    normed = normed_ref[...]
    cotangent = cotangent_ref[...]
    turned = turned_ref[...]
    sides = sides_ref[...]
    part = gate_ref.shape[1]
    size = part
    output, back_sum = sum_ref[...], back_ref[...]
    grads, mixes = [], []
    for begin in range(0, part, size):
        here = slice(begin, begin + size)
        gate = plain_dot(normed, gate_ref[:, here])
        up = plain_dot(normed, up_ref[:, here])
        back = rows_dot(cotangent, down_ref[here, :])
        square = gate * gate
        curve = jnp.tanh(gelu_scale * (gate + gelu_cubic * gate * square))
        half = 0.5 * (1.0 + curve)
        bent = gate * half
        slope = half + 0.5 * gate * (1.0 - curve * curve) * (
            gelu_scale * (1.0 + 3.0 * gelu_cubic * square)
        )
        mixed = (bent * up).astype(low)
        grad_gate = (back * up * slope).astype(low)
        grad_up = (back * bent).astype(low)
        output = output + plain_dot(mixed, down_ref[here, :])
        back_sum = (
            back_sum
            + rows_dot(grad_gate, gate_ref[:, here])
            + rows_dot(grad_up, up_ref[:, here])
        )
        mixes.append(mixed)
        grads.append((grad_gate, grad_up))
    sum_ref[...] = output
    back_ref[...] = back_sum
    side = (step >> 1) * parcel.own
    for kind, (side_ref, target_ref) in enumerate(
        ((kept_ref, kept_out_ref), (sent_ref, sent_out_ref))
    ):

        @pl.when(((step & 1) ^ core) == kind)
        def _():
            for job in (0, 1):
                rows = parcel.heights[job]
                for which, pair in enumerate(grads):
                    product = plain_dot(turned, pair[job]).astype(low)
                    for tile in range(size // LANES):
                        at = side + parcel.at[job] + (which * size // LANES + tile) * rows
                        at = pl.multiple_of(at, 16)
                        for block in range(BLOCKS):
                            side_ref[place(block), pl.ds(at, rows), :] = product[
                                block * rows : (block + 1) * rows, tile * LANES : (tile + 1) * LANES
                            ]
            copies(side_ref, target_ref, pl.multiple_of(side, 16), inner, step).start()

    rows = parcel.heights[2]
    tiles = sides.shape[1] // LANES // 2
    for which, mixed in enumerate(mixes):
        product = cols_dot(mixed, sides).astype(low)
        here = product.shape[0] // rows
        for kind, side_ref in enumerate((kept_ref, sent_ref)):
            for tile in range(tiles):
                lane = (kind * tiles + tile) * LANES
                for block in range(here):
                    put_block(
                        parcel,
                        2,
                        tile,
                        product[block * rows : (block + 1) * rows, lane : lane + LANES],
                        side_ref,
                        place(step * here + block),
                    )

    @pl.when(step == pl.num_programs(0) - 1)
    def _():
        hidden = hidden_ref[...]
        result_ref[...] = sum_ref[...].astype(low)
        to_rows, to_gain = norm_back(hidden, gain, back_ref[...])
        grad_gain_ref[...] = to_gain
        grad_hidden = cotangent.astype(high) + to_rows
        grad_hidden_ref[...] = grad_hidden
        branch = grad_hidden.astype(low)
        branch_ref[...] = branch
        grad_crossed_ref[...] = rows_dot(branch, out_ref[...]).astype(low)
        sides = jnp.concatenate(both_sides(branch, core), axis=1)
        product = cols_dot(crossed_ref[...], sides).astype(low)
        for kind, side_ref in enumerate((kept_ref, sent_ref)):
            for tile in range(tiles):
                put_rows(parcel, 3, product, tile, side_ref, kind * tiles + tile)
        spans = ((inner, parcel.own), (parcel.own + inner, parcel.rows))
        last = [
            copies(side_ref, target_ref, begin, end - begin, parts + 2 * kind + which)
            for kind, (side_ref, target_ref) in enumerate(
                ((kept_ref, kept_out_ref), (sent_ref, sent_out_ref))
            )
            for which, (begin, end) in enumerate(spans)
        ]
        for copy in last:
            copy.start()
        for slot in range(parts):
            copies(kept_ref, kept_out_ref, 0, inner, slot).wait()
        for copy in last:
            copy.wait()


def feed_call(
    parcel, core, crossed, hidden, cotangent, gain, out_weight, gate_weight, up_weight, down_weight
):
    tokens, width = crossed.shape
    inner = gate_weight.shape[1]
    parts = lax.axis_size("narrow")
    part = inner // parts
    whole = lambda piece: whole_spec(piece.shape)
    fixed = lambda shape: pl.BlockSpec(shape, lambda step: (0,) * len(shape))
    parcel_shape = (BLOCKS, parcel.rows, LANES)
    return pl.pallas_call(
        lambda *refs: feed_both(parcel, parts, *refs),
        grid=(parts,),
        in_specs=[pl.BlockSpec(memory_space=pltpu.SMEM)]
        + [whole(crossed), whole(hidden), whole(cotangent), whole(gain), whole(out_weight)]
        + [pl.BlockSpec((width, part), lambda step: (0, step))] * 2
        + [pl.BlockSpec((part, width), lambda step: (step, 0))],
        out_specs=[fixed((tokens, width))] * 4
        + [fixed((1, width))]
        + [pl.BlockSpec(memory_space=pl.ANY)] * 2,
        out_shape=[
            jax.ShapeDtypeStruct((tokens, width), low),
            jax.ShapeDtypeStruct((tokens, width), high),
            jax.ShapeDtypeStruct((tokens, width), low),
            jax.ShapeDtypeStruct((tokens, width), low),
            jax.ShapeDtypeStruct((1, width), high),
            jax.ShapeDtypeStruct(parcel_shape, low),
            jax.ShapeDtypeStruct(parcel_shape, low),
        ],
        scratch_shapes=[
            pltpu.VMEM((tokens, width), high),
            pltpu.VMEM((tokens, width), low),
            pltpu.VMEM((width, tokens), low),
            pltpu.VMEM((tokens, width), high),
            pltpu.VMEM((tokens, width), high),
            pltpu.VMEM((tokens, width), low),
            pltpu.VMEM(parcel_shape, low),
            pltpu.VMEM(parcel_shape, low),
            pltpu.SemaphoreType.DMA((parts + 4,)),
        ],
        cost_estimate=cost("feed_both"),
        compiler_params=pltpu.CompilerParams(vmem_limit_bytes=vmem_bytes),
        name="feed_both",
    )(core, crossed, hidden, cotangent, gain, out_weight, gate_weight, up_weight, down_weight)


def lower_bits(sums):
    levels = lax.axis_size("items").bit_length() - 1
    for bit in range(levels - 4, -1, -1):
        mine = bit_of("items", bit)
        halves = [piece.reshape(2, piece.shape[0] // 2, piece.shape[1]) for piece in sums]
        sums = [pick(piece, mine) + swap(pick(piece, 1 - mine), "items", 1 << bit) for piece in halves]
    return sums


def memory_back(parcel, core_ref, *refs):
    wk_ref, wv_ref, away_ref, near_ref, kept_ref, sent_ref, total_ref = refs[6:]
    step = pl.program_id(0)
    steps = pl.num_programs(0)

    def block(rows_ref, grad_k_ref, grad_v_ref, grad_ref, first):
        grad_k, grad_v = grad_k_ref[...], grad_v_ref[...]
        grad_ref[...] = (rows_dot(grad_k, wk_ref[...]) + rows_dot(grad_v, wv_ref[...])).astype(low)
        width = grad_k.shape[1]
        rows = rows_ref[...].T
        parts = plain_dot(rows, grad_k), plain_dot(rows, grad_v)
        for job, part in enumerate(parts):
            columns = slice(job * width, (job + 1) * width)

            if first:

                @pl.when(step == 0)
                def _():
                    total_ref[:, columns] = part

                @pl.when(step > 0)
                def _():
                    total_ref[:, columns] += part

            else:
                total_ref[:, columns] += part

    @pl.when(step < steps // 2)
    def _():
        block(*refs[:3], away_ref, True)

    @pl.when(step >= steps // 2)
    def _():
        block(*refs[3:6], near_ref, False)

    @pl.when(step == steps - 1)
    def _():
        core = core_ref[0]
        for job, (_, width) in enumerate(parcel.shapes):
            total = total_ref[:, job * width : (job + 1) * width].astype(low)
            tiles = both_sides(total, core)
            count = len(tiles) // 2
            for at, product in enumerate(tiles):
                kind, tile = divmod(at, count)
                put_rows(parcel, job, product, tile, (kept_ref, sent_ref)[kind], 0)


def memory_back_call(parcel, core, far, near, wk, wv):
    total, width = far[0].shape
    half = total // 2
    name = "memory_back"
    first = lambda: pl.BlockSpec((half, width), lambda step: (jnp.minimum(step, 1), 0))
    second = lambda: pl.BlockSpec((half, width), lambda step: (jnp.maximum(step - 2, 0), 0))
    parcel_shape = (BLOCKS, parcel.rows, LANES)
    fixed = pl.BlockSpec(parcel_shape, lambda step: (0, 0, 0))
    return pl.pallas_call(
        lambda *refs: memory_back(parcel, *refs),
        grid=(4,),
        in_specs=[pl.BlockSpec(memory_space=pltpu.SMEM)]
        + [first() for _ in far]
        + [second() for _ in near]
        + [whole_spec(piece.shape) for piece in (wk, wv)],
        out_specs=[first(), second(), fixed, fixed],
        out_shape=[jax.ShapeDtypeStruct((total, width), low)] * 2
        + [jax.ShapeDtypeStruct(parcel_shape, low)] * 2,
        scratch_shapes=[pltpu.VMEM((width, 2 * width), high)],
        cost_estimate=cost(name),
        compiler_params=pltpu.CompilerParams(vmem_limit_bytes=vmem_bytes),
        name=name,
    )(core, *far, *near, wk, wv)


def land_memory(place_ref, *refs):
    for which in range(len(refs) - 1):

        @pl.when(pl.program_id(0) == which)
        def _():
            refs[-1][0] = refs[which][...].astype(high)


def land_call(place, pieces):
    rows, width = pieces[1].shape
    return pl.pallas_call(
        land_memory,
        out_shape=jax.ShapeDtypeStruct((len(pieces), rows, width), high),
        grid_spec=pltpu.PrefetchScalarGridSpec(
            num_scalar_prefetch=1,
            grid=(len(pieces),),
            in_specs=[
                pl.BlockSpec((rows, width), lambda step, _: (0, 0), pipeline_mode=pl.Buffered(1))
                for _ in pieces
            ],
            out_specs=pl.BlockSpec((1, rows, width), lambda step, place: (place[0] ^ step, 0, 0)),
        ),
        cost_estimate=cost("land_memory"),
        compiler_params=pltpu.CompilerParams(vmem_limit_bytes=vmem_bytes),
        name="land_memory",
    )(place, *pieces)


def two_heads(rows):
    first = lax.broadcasted_iota(jnp.int32, rows.shape, 1) < HD
    zero = jnp.zeros_like(rows)
    return jnp.concatenate([jnp.where(first, rows, zero), jnp.where(first, zero, rows)], axis=0)


def one_pair(stacked):
    half = stacked.shape[1] // 2
    first = lax.broadcasted_iota(jnp.int32, (stacked.shape[0], half), 0) < HD
    return jnp.where(first, stacked[:, :half], stacked[:, half:]).T


def attend_forward_kernel(causal, chunks, carried, last, live_ref, q_ref, k_ref, v_ref, *refs):
    before, refs = refs[:carried], refs[carried:]
    queries = two_heads(q_ref[...])
    wide = queries.shape[0]
    size = k_ref.shape[0] // chunks

    def weigh(here, scores, peak):
        weights = jnp.exp(scores - peak)
        total = jnp.sum(weights, axis=0, keepdims=True)
        weights = weights.astype(low)
        refs[0][0, here, :] = weights
        return total, cols_dot(v_ref[here, :], weights)

    stats_ref, mixed_ref = refs[-2:]
    squares = queries.astype(high)
    squares = (squares * squares).astype(low)
    lengths = rows_dot(jnp.ones((8, LANES), low), squares)[:1]
    if not causal:
        lane = lax.broadcasted_iota(jnp.int32, queries.shape, 1)
        queries = jnp.concatenate([queries, jnp.where(lane == 0, 1.0, 0.0).astype(low)], axis=1)
    for chunk in range(chunks):
        here = slice(chunk * size, (chunk + 1) * size)
        live = size if causal else live_ref[chunk + (chunks if carried else 0)]

        def scored():
            keys = k_ref[here, :]
            if causal:
                key = lax.broadcasted_iota(jnp.int32, (size, wide), 0) + chunk * size
                token = lax.broadcasted_iota(jnp.int32, (size, wide), 1)
                token = jnp.where(token >= wide // 2, token - wide // 2, token)
                return jnp.where(key <= token, rows_dot(keys, queries), neg_big)
            key = lax.broadcasted_iota(jnp.int32, keys.shape, 0)
            lane = lax.broadcasted_iota(jnp.int32, keys.shape, 1)
            dead = jnp.where((lane == 0) & (key >= live), neg_big, 0.0).astype(low)
            return rows_dot(jnp.concatenate([keys, dead], axis=1), queries)

        def keep(scores, peak):
            total, mix = weigh(here, scores, peak)
            stats_ref[chunk : chunk + 1, :] = peak if causal else jnp.where(live > 0, peak, neg_big)
            stats_ref[chunks + chunk : chunks + chunk + 1, :] = total
            mixed_ref[chunk] = mix
            return total

        squares = k_ref[here, :].astype(high)
        squares = squares * squares
        first = lax.broadcasted_iota(jnp.int32, squares.shape, 1) < HD
        sides = [
            jnp.max(jnp.sum(jnp.where(side, squares, 0.0), axis=1, keepdims=True), axis=0, keepdims=True)
            for side in (first, ~first)
        ]
        column = lax.broadcasted_iota(jnp.int32, (1, wide), 1)
        longest = jnp.where(column < wide // 2, sides[0], sides[1])
        total = keep(scored(), 1.01 * jnp.sqrt(lengths * longest))

        @pl.when((live > 0) & (jnp.min(total) < smallest_total))
        def _():
            scores = scored()
            keep(scores, jnp.max(scores, axis=0, keepdims=True))

    peaks = [stats_ref[at : at + 1] for at in range(chunks)]
    totals = [stats_ref[chunks + at : chunks + at + 1] for at in range(chunks)]
    mixes = [mixed_ref[at] for at in range(chunks)]
    if carried:
        stats_in = before[1][0]
        count = chunks
        peaks = [stats_in[at : at + 1] for at in range(count)] + peaks
        totals = [stats_in[count + at : count + at + 1] for at in range(count)] + totals
    top = peaks[0]
    for peak in peaks[1:]:
        top = jnp.maximum(top, peak)
    scales = [jnp.exp(peak - top) for peak in peaks]
    mixed = sum(mix * scale for mix, scale in zip(mixes, scales[-chunks:]))
    if carried:
        earlier = peaks[0]
        for peak in peaks[1:chunks]:
            earlier = jnp.maximum(earlier, peak)
        mixed = mixed + before[0][0] * jnp.exp(earlier - top)
    if last:
        inverse = 1.0 / sum(total * scale for total, scale in zip(totals, scales))
        refs[1][...] = one_pair(mixed * inverse).astype(low)
        for at, scale in enumerate(scales):
            refs[2][0, at : at + 1, :] = scale * inverse
    else:
        refs[1][0] = mixed
        for at in range(chunks):
            refs[2][0, at : at + 1, :] = peaks[at]
            refs[2][0, chunks + at : chunks + at + 1, :] = totals[at]


def attend_forward(queries, keys, values, live, causal, chunks, name, last=True, before=()):
    tokens, width = queries.shape
    patches = keys.shape[0]
    pairs = width // LANES
    by_pair = lambda rows: pl.BlockSpec((rows, LANES), lambda pair, _: (0, pair))
    stack = lambda rows: pl.BlockSpec((1, rows, 2 * tokens), lambda pair, _: (pair, 0, 0))
    return pl.pallas_call(
        lambda *refs: attend_forward_kernel(causal, chunks, len(before), last, *refs),
        out_shape=(
            jax.ShapeDtypeStruct((pairs, patches, 2 * tokens), low),
            jax.ShapeDtypeStruct((tokens, width), low)
            if last
            else jax.ShapeDtypeStruct((pairs, LANES, 2 * tokens), high),
            jax.ShapeDtypeStruct((pairs, 8, 2 * tokens), high),
        ),
        grid_spec=pltpu.PrefetchScalarGridSpec(
            num_scalar_prefetch=1,
            grid=(pairs,),
            in_specs=[by_pair(tokens), by_pair(patches), by_pair(patches)]
            + [stack(piece.shape[1]) for piece in before],
            out_specs=[stack(patches), by_pair(tokens) if last else stack(LANES), stack(8)],
            scratch_shapes=[
                pltpu.VMEM((2 * chunks, 2 * tokens), high),
                pltpu.VMEM((chunks, LANES, 2 * tokens), high),
            ],
        ),
        cost_estimate=cost(name),
        compiler_params=pltpu.CompilerParams(vmem_limit_bytes=vmem_bytes),
        name=name,
    )(live, queries, keys, values, *before)


def attend_backward_kernel(
    chunks,
    offset,
    carried,
    last,
    weight_ref,
    inverse_ref,
    q_ref,
    k_ref,
    v_ref,
    mixed_ref,
    grad_mixed_ref,
    *refs,
):
    before, (grad_q_ref, grad_k_ref, grad_v_ref) = refs[:carried], refs[-3:]
    queries = two_heads(q_ref[...])
    grads = grad_mixed_ref[...].astype(high).T
    mixed = mixed_ref[...].astype(high).T
    first = lax.broadcasted_iota(jnp.int32, grads.shape, 0) < HD
    zero = jnp.zeros_like(grads)
    grads = jnp.concatenate([jnp.where(first, grads, zero), jnp.where(first, zero, grads)], axis=1)
    mixed = jnp.concatenate([mixed, mixed], axis=1)
    size = k_ref.shape[0] // chunks
    grad_q = jnp.zeros(grads.shape, high)
    for chunk in range(chunks):
        here = slice(chunk * size, (chunk + 1) * size)
        at = offset + chunk
        scaled = (grads * inverse_ref[0, at : at + 1, :]).astype(low)
        wide = scaled.astype(high)
        centre = jnp.sum(wide * mixed, axis=0, keepdims=True)
        rows = wide.T.astype(low)
        weights = weight_ref[0, here, :]
        grad_probs = plain_dot(v_ref[here, :], scaled)
        grad_scores = (weights.astype(high) * (grad_probs - centre)).astype(low)
        grad_v_ref[here, :] = plain_dot(weights, rows).astype(low)
        grad_k_ref[here, :] = plain_dot(grad_scores, queries).astype(low)
        grad_q = grad_q + cols_dot(k_ref[here, :], grad_scores)
    grad_q = one_pair(grad_q)
    if carried:
        grad_q = grad_q + before[0][...]
    grad_q_ref[...] = grad_q.astype(grad_q_ref.dtype)


def attend_backward(
    weights,
    inverse,
    queries,
    keys,
    values,
    mixed,
    grad_mixed,
    chunks,
    offset,
    name,
    last=True,
    before=(),
    pairs=None,
    filled=(),
):
    tokens, width = queries.shape
    patches = keys.shape[0]
    begin, end = pairs or (0, width // LANES)
    by_token = pl.BlockSpec((tokens, LANES), lambda pair: (0, pair + begin))
    by_patch = pl.BlockSpec((patches, LANES), lambda pair: (0, pair + begin))
    return pl.pallas_call(
        lambda *refs: attend_backward_kernel(chunks, offset, len(before), last, *refs),
        out_shape=(
            jax.ShapeDtypeStruct((tokens, width), low if last else high),
            jax.ShapeDtypeStruct((patches, width), low),
            jax.ShapeDtypeStruct((patches, width), low),
        ),
        grid=(end - begin,),
        in_specs=[
            pl.BlockSpec((1, patches, 2 * tokens), lambda pair: (pair + begin, 0, 0)),
            pl.BlockSpec((1, 8, 2 * tokens), lambda pair: (pair + begin, 0, 0)),
            by_token,
            by_patch,
            by_patch,
            by_token,
            by_token,
        ]
        + [by_token] * len(before)
        + [pl.BlockSpec(memory_space=pl.ANY)] * len(filled),
        out_specs=[by_token, by_patch, by_patch],
        input_output_aliases={7 + len(before) + which: which for which in range(len(filled))},
        cost_estimate=cost(name),
        compiler_params=pltpu.CompilerParams(vmem_limit_bytes=vmem_bytes),
        name=name,
    )(weights, inverse, queries, keys, values, mixed, grad_mixed, *before, *filled)


def swap(piece, axis_name, mask):
    size = lax.axis_size(axis_name)
    return lax.ppermute(piece, axis_name, [(place, place ^ mask) for place in range(size)])


def bit_of(axis_name, bit):
    return (lax.axis_index(axis_name) >> bit) & 1


def pick(piece, which):
    return lax.dynamic_index_in_dim(piece, which, 0, keepdims=False)


class Parcel:
    def __init__(self, shapes, extra=0):
        self.shapes = shapes
        self.heights = [height // BLOCKS for height, _ in shapes]
        self.plain = [width // 4 // LANES for _, width in shapes]
        self.at = []
        at = 0
        for (_, width), tiles, height in zip(shapes, self.plain, self.heights):
            self.at.append(at)
            at += tiles * height + (height // 2 if width // 4 % LANES else 0)
        self.extra = extra
        self.own = at + extra
        self.rows = 2 * self.own


def place(block):
    return (block & 1) * 4 + (block & 2) + (block >> 2)


def core_tiles(grad, core):
    quarter = grad.shape[1] // 4
    starts = [core * quarter, 2 * quarter + core * quarter]
    tiles = [
        grad[:, start + at : start + at + LANES]
        for start in starts
        for at in range(0, quarter - LANES + 1, LANES)
    ]
    rest = quarter % LANES
    if rest:
        tiles.append(
            jnp.concatenate(
                [grad[:, start + quarter - rest : start + quarter] for start in starts], axis=1
            )
        )
    return tiles


def both_sides(grad, core):
    first, second = core_tiles(grad, 0), core_tiles(grad, 1)
    own = [jnp.where(core == 0, one, other) for one, other in zip(first, second)]
    return own + [jnp.where(core == 0, other, one) for one, other in zip(first, second)]


def self_backward(
    parcel,
    core_ref,
    grad_q_two_ref,
    hidden_ref,
    grad_in_ref,
    gain_ref,
    cross_query_ref,
    out_weight_ref,
    feed_gain_ref,
    attended_ref,
    weight_ref,
    inverse_ref,
    q_ref,
    k_ref,
    v_ref,
    mixed_ref,
    wq_ref,
    wk_ref,
    wv_ref,
    normed_hbm_ref,
    next_normed_hbm_ref,
    tokens_hbm_ref,
    tokens_grad_ref,
    kept_ref,
    sent_ref,
    grad_hidden_ref,
    branch_ref,
    grad_mixed_ref,
    gains_ref,
    grads_ref,
    back_ref,
    late_ref,
    turned_ref,
    packed_ref,
    done_ref,
):
    pair = pl.program_id(0)
    pairs = pl.num_programs(0)
    late = [
        pltpu.make_async_copy(far_ref, late_ref.at[at], done_ref.at[at])
        for at, far_ref in enumerate((normed_hbm_ref, next_normed_hbm_ref, tokens_hbm_ref))
    ]

    @pl.when(pair == 0)
    def _():
        for copy in late:
            copy.start()
        to_rows, to_gain = norm_back(
            hidden_ref[...], gain_ref[1:2, :], rows_dot(grad_q_two_ref[...], cross_query_ref[...])
        )
        grad_hidden = grad_in_ref[...] + to_rows
        grad_hidden_ref[...] = grad_hidden
        branch = grad_hidden.astype(low)
        branch_ref[...] = branch
        grad_mixed_ref[...] = rows_dot(branch, out_weight_ref[...]).astype(low)
        gains_ref[1:2, :] = to_gain
        gains_ref[2:3, :] = feed_gain_ref[...]
        back_ref[...] = jnp.zeros_like(back_ref)

    here = pl.ds(pl.multiple_of(pair * LANES, LANES), LANES)
    views = [grads_ref.at[at, :, here] for at in range(3)]
    attend_backward_kernel(
        1,
        0,
        0,
        True,
        weight_ref,
        inverse_ref,
        q_ref,
        k_ref,
        v_ref,
        mixed_ref,
        grad_mixed_ref.at[:, here],
        *views,
    )
    grads = jnp.concatenate([view[...] for view in views], axis=1)
    weights = jnp.concatenate([wq_ref[...], wk_ref[...], wv_ref[...]], axis=1)
    back_ref[...] += rows_dot(grads, weights)

    @pl.when(pair == pairs - 1)
    def _():
        for copy in late:
            copy.wait()
        to_rows, to_gain = norm_back(late_ref[2].astype(high), gain_ref[0:1, :], back_ref[...])
        tokens_grad_ref[...] = (grad_hidden_ref[...] + to_rows).astype(low)
        gains_ref[0:1, :] = to_gain
        width = to_gain.shape[1]
        tiles = width // LANES
        packed_ref[...] = jnp.zeros_like(packed_ref)
        for gain in range(3):
            for tile in range(tiles):
                packed_ref[gain * tiles + tile : gain * tiles + tile + 1, :] = gains_ref[
                    gain : gain + 1, tile * LANES : (tile + 1) * LANES
                ]
        packed = packed_ref[...].astype(low)
        for out_ref in (kept_ref, sent_ref):
            for block in range(BLOCKS):
                for end in (parcel.own, parcel.rows):
                    out_ref[block, end - parcel.extra : end, :] = packed
        core = core_ref[0]
        jobs = (
            [(late_ref.at[0], grads_ref[at]) for at in range(3)]
            + [(late_ref.at[1], grad_q_two_ref[...])]
            + [(attended_ref, branch_ref[...])]
        )
        for job, (rows_ref, grad) in enumerate(jobs):
            if job in (0, 3, 4):
                turned_ref[...] = rows_ref[...].T
            tiles = both_sides(grad, core)
            count = len(tiles) // 2
            for begin in range(0, 2 * count, 2):
                product = plain_dot(
                    turned_ref[...], jnp.concatenate(tiles[begin : begin + 2], axis=1)
                ).astype(low)
                for slot in (0, 1):
                    kind, tile = divmod(begin + slot, count)
                    put_rows(parcel, job, product, tile, (kept_ref, sent_ref)[kind], slot)


def self_backward_call(
    parcel,
    core,
    grad_q_two,
    hidden,
    grad_in,
    gain,
    cross_query,
    out_weight,
    feed_gain,
    attended,
    weights,
    inverse,
    queries,
    keys,
    values,
    projections,
    late,
):
    rows, width = hidden.shape
    pairs = width // LANES
    columns = pl.BlockSpec((rows, LANES), lambda pair: (0, pair))
    stack = lambda height: pl.BlockSpec((1, height, 2 * rows), lambda pair: (pair, 0, 0))
    whole = (grad_q_two, hidden, grad_in, gain, cross_query, out_weight, feed_gain, attended)
    fixed = lambda shape: pl.BlockSpec(shape, lambda pair: (0,) * len(shape))
    parcel_shape = (BLOCKS, parcel.rows, LANES)
    return pl.pallas_call(
        lambda *refs: self_backward(parcel, *refs),
        grid=(pairs,),
        in_specs=[pl.BlockSpec(memory_space=pltpu.SMEM)]
        + [whole_spec(piece.shape) for piece in whole]
        + [stack(rows), stack(8), columns, columns, columns, columns]
        + [pl.BlockSpec((width, LANES), lambda pair: (0, pair))] * 3
        + [pl.BlockSpec(memory_space=pl.ANY)] * 3,
        out_specs=[fixed((rows, width)), whole_spec(parcel_shape), whole_spec(parcel_shape)],
        out_shape=[
            jax.ShapeDtypeStruct((rows, width), low),
            jax.ShapeDtypeStruct(parcel_shape, low),
            jax.ShapeDtypeStruct(parcel_shape, low),
        ],
        scratch_shapes=[
            pltpu.VMEM((rows, width), high),
            pltpu.VMEM((rows, width), low),
            pltpu.VMEM((rows, width), low),
            pltpu.VMEM((8, width), high),
            pltpu.VMEM((3, rows, width), low),
            pltpu.VMEM((rows, width), high),
            pltpu.VMEM((3, rows, width), low),
            pltpu.VMEM((width, rows), low),
            pltpu.VMEM((parcel.extra, LANES), high),
            pltpu.SemaphoreType.DMA((3,)),
        ],
        cost_estimate=cost("self_backward"),
        compiler_params=pltpu.CompilerParams(vmem_limit_bytes=vmem_bytes),
        name="self_backward",
    )(
        core,
        *whole,
        weights,
        inverse,
        queries,
        keys,
        values,
        attended,
        *projections,
        *late,
    )


def fold_one(mine_ref, kept_ref, received_ref, *out_refs):
    for which, out_ref in enumerate(out_refs):

        @pl.when(pl.program_id(0) == which)
        def _():
            total = kept_ref[0].astype(high) + received_ref[0].astype(high)
            out_ref[...] = total.astype(low)


def fold_one_call(name, mine, kept, received, view, shape, index):
    block = pl.BlockSpec((1, *shape), lambda step, mine: index(mine[0] ^ step))
    return pl.pallas_call(
        fold_one,
        grid_spec=pltpu.PrefetchScalarGridSpec(
            num_scalar_prefetch=1,
            grid=(4,),
            in_specs=[block, block],
            out_specs=[
                pl.BlockSpec(shape, lambda step, _: (0, 0, 0), pipeline_mode=pl.Buffered(1))
            ]
            * 4,
        ),
        out_shape=[jax.ShapeDtypeStruct(shape, low)] * 4,
        cost_estimate=cost(name),
        compiler_params=pltpu.CompilerParams(vmem_limit_bytes=vmem_bytes),
        name=name,
    )(mine, kept.reshape(view), received.reshape(view))


def sum_of(refs):
    first, second, third, fourth = [ref[...].astype(high) for ref in refs]
    return (first + second) + (third + fourth)


def fold_two(parcel, with_x, first_ref, second_ref, third_ref, fourth_ref, out_ref):
    total = sum_of((first_ref, second_ref, third_ref, fourth_ref)).astype(low)
    if with_x:
        out_ref[...] = total
    else:
        for which in range(4):
            begin = (which & 1) * parcel.own
            out_ref[which] = total[which >> 1, begin : begin + parcel.own, :]


def fold_end(parcel, parts_ref, *outs):
    total = sum_of([parts_ref.at[which] for which in range(4)])
    for job, rows in enumerate(parcel.heights):
        at = parcel.at[job]
        for tile in range(parcel.plain[job]):
            outs[job][:, tile * LANES : (tile + 1) * LANES] = total[at : at + rows]
            at += rows
        begin = parcel.plain[job] * LANES
        rest = outs[job].shape[1] - begin
        if rest:
            outs[job][: rows // 2, begin:] = total[at : at + rows // 2, :rest]
            outs[job][rows // 2 :, begin:] = total[at : at + rows // 2, rest:]
    if parcel.extra:
        outs[-1][...] = total[-parcel.extra :]


class Travel:
    def __init__(self, parcel, kept, sent, name, with_x):
        self.parcel = parcel
        self.name = name
        self.kept = kept
        self.received = swap(sent, "narrow", 1)
        self.top = lax.axis_size("items").bit_length() - 4
        self.with_x = with_x

    def joint(self, up, side):
        narrow = lax.axis_size("narrow")
        return [
            (place, ((place // narrow) ^ up) * narrow + ((place % narrow) ^ side))
            for place in range(lax.axis_size("items") * narrow)
        ]

    def fold_one(self, *earlier):
        kept, received = lax.optimization_barrier((self.kept, self.received, *earlier))[:2]
        rows, top = self.parcel.rows, self.top
        if self.with_x:
            mine = bit_of("items", top) * 2 + bit_of("narrow", 1)
            view, shape = (2, 4, rows, LANES), (4, self.parcel.own, LANES)
            partners = [(0, 2), (1 << top, 0), (1 << top, 2)]
            index = lambda part: (part >> 1, 0, part & 1, 0)
        else:
            mine = bit_of("items", top) * 2 + bit_of("items", top + 1)
            view, shape = (4, 2, rows, LANES), (2, rows, LANES)
            partners = [(2 << top, 0), (1 << top, 0), (3 << top, 0)]
            index = lambda part: (part, 0, 0, 0)
        parts = fold_one_call(
            self.name + "_one", mine.reshape(1), kept, received, view, shape, index
        )
        self.parts = [parts[0]] + [
            lax.ppermute(part, ("items", "narrow"), self.joint(*partner))
            for part, partner in zip(parts[1:], partners)
        ]
        return parts[0]

    def fold_two(self, *earlier):
        parts = lax.optimization_barrier((*self.parts, *earlier))[:4]
        parcel = self.parcel
        (parts,) = one_step_call(
            lambda *refs: fold_two(parcel, self.with_x, *refs),
            self.name + "_two",
            list(parts),
            [((4, parcel.own, LANES), low)],
        )
        far = 4 << self.top
        first, second = ((2 << self.top, 0), (far, 0)) if self.with_x else ((far, 0), (0, 2))
        narrow = lax.axis_size("narrow")
        clear = first[0] | second[0]
        side = first[1] | second[1]
        groups = [
            [
                (item | one[0] | two[0]) * narrow + (other | one[1] | two[1])
                for one in ((0, 0), first)
                for two in ((0, 0), second)
            ]
            for item in range(lax.axis_size("items"))
            for other in range(narrow)
            if not item & clear and not other & side
        ]
        self.parts = parts
        self.groups = groups
        return parts

    def send(self, *earlier):
        parts = lax.optimization_barrier((self.parts, *earlier))[0]
        self.parts = lax.all_to_all(
            parts, ("items", "narrow"), 0, 0, axis_index_groups=self.groups, tiled=True
        )

    def end(self, *earlier):
        parts = lax.optimization_barrier((self.parts, *earlier))[0]
        parcel = self.parcel
        outs = [((height // BLOCKS, width // 4), high) for height, width in parcel.shapes]
        outs += [((parcel.extra, LANES), high)] if parcel.extra else []
        outs = list(
            one_step_call(
                lambda *refs: fold_end(parcel, *refs),
                self.name + "_end",
                [parts],
                outs,
            )
        )
        count = len(parcel.shapes)
        extras = outs[count:]
        for bit in range(self.top, 0, -1):
            extras = [piece + swap(piece, "items", 1 << (bit - 1)) for piece in extras]
        return list(lower_bits(outs[:count])) + extras


def exchange(piece):
    return lax.all_to_all(piece, "narrow", split_axis=0, concat_axis=0, tiled=True)


def body(
    tokens,
    memory,
    mem_count,
    cotangent,
    gain_self,
    self_query,
    self_key,
    self_value,
    self_out,
    gain_cross,
    cross_query,
    cross_key,
    cross_value,
    cross_out,
    gain_feed,
    gate_weight,
    up_weight,
    down_weight,
):
    width = tokens.shape[2]
    inner = gate_weight.shape[1]
    gains_in = jnp.stack([gain_self, gain_cross, gain_feed])
    parts = lax.axis_size("narrow")
    mine = lax.axis_index("narrow")
    token_rows = exchange(tokens).reshape(-1, width)
    own_memory, *away_memory = [pick(memory, mine ^ which) for which in range(parts)]
    pieces = [own_memory] + [
        swap(piece, "narrow", which + 1) for which, piece in enumerate(away_memory)
    ]
    cotangent_rows = exchange(cotangent).reshape(-1, width)
    count = pick(mem_count, mine)
    local_mem = memory.shape[1]
    live = count - local_mem * (mine ^ jnp.arange(parts, dtype=jnp.int32))
    kinds = [((2 * local_mem, width), low)] * 3
    near_rows, near_keys, near_values = one_step_call(
        enter_memory,
        "enter_memory_near",
        [pieces[0], pieces[1], cross_key, cross_value],
        kinds,
    )
    (
        normed_one,
        query_one,
        key_one,
        value_one,
        weights_one,
        attended,
        inverse_one,
        hidden_one,
        normed_two,
        query_two,
    ) = self_forward_call(
        after(token_rows, near_keys),
        gains_in,
        cross_query,
        self_query,
        self_key,
        self_value,
        self_out,
    )
    near_weights, near_mixed, near_stats = attend_forward(
        query_two, near_keys, near_values, live, False, 2, "cross_forward_near", False
    )
    far_rows, far_keys, far_values = one_step_call(
        enter_memory,
        "enter_memory_far",
        [after(pieces[2], near_stats), pieces[3], cross_key, cross_value],
        kinds,
    )
    far_weights, crossed, inverse_two = attend_forward(
        query_two,
        far_keys,
        far_values,
        live,
        False,
        2,
        "cross_forward_far",
        True,
        (near_mixed, near_stats),
    )
    square = (width, width)
    feed_parcel = Parcel([(width, inner), (width, inner), (inner, width), square])
    result, grad_hidden_two, branch_two, grad_crossed, grad_gain_feed, *feed_parts = feed_call(
        feed_parcel,
        bit_of("narrow", 0).reshape(1),
        crossed,
        hidden_one,
        cotangent_rows,
        gains_in,
        cross_out,
        gate_weight,
        up_weight,
        down_weight,
    )
    feed_trip = Travel(feed_parcel, *feed_parts, "feed_weights", True)
    result = exchange(result.reshape(tokens.shape))
    far = ()
    ready = feed_trip.kept
    for pairs in ((0, 3), (3, 6)):
        far = attend_backward(
            far_weights,
            inverse_two,
            query_two,
            far_keys,
            far_values,
            crossed,
            after(grad_crossed, ready),
            2,
            2,
            "cross_backward_far_a" if pairs[0] == 0 else "cross_backward_far_b",
            False,
            pairs=pairs,
            filled=far,
        )
        ready = feed_trip.fold_one(far[0]) if pairs[0] == 0 else far[0]
    far_grad_q, far_grad_k, far_grad_v = far
    grad_query_two, near_grad_k, near_grad_v = attend_backward(
        near_weights,
        inverse_two,
        query_two,
        near_keys,
        near_values,
        crossed,
        after(grad_crossed, result),
        2,
        0,
        "cross_backward_near",
        True,
        (far_grad_q,),
    )
    extra = -(-3 * width // LANES // 16) * 16
    self_parcel = Parcel([square] * 5, extra)
    tokens_grad, *self_parts = self_backward_call(
        self_parcel,
        bit_of("narrow", 0).reshape(1),
        grad_query_two,
        hidden_one,
        grad_hidden_two,
        gains_in,
        cross_query,
        self_out,
        grad_gain_feed,
        attended,
        weights_one,
        inverse_one,
        query_one,
        key_one,
        value_one,
        [self_query, self_key, self_value],
        [normed_one, normed_two, token_rows],
    )
    self_trip = Travel(self_parcel, *self_parts, "self_weights", True)
    tokens_grad = exchange(tokens_grad.reshape(tokens.shape))
    ready = feed_trip.fold_two(self_parts[0])
    feed_trip.send()
    ready = self_trip.fold_one(ready)
    cross_parcel = Parcel([square] * 2)
    grad_away, grad_near, *cross_parts = memory_back_call(
        cross_parcel,
        bit_of("narrow", 0).reshape(1),
        [after(far_rows, ready, tokens_grad), far_grad_k, far_grad_v],
        [near_rows, near_grad_k, near_grad_v],
        cross_key,
        cross_value,
    )
    landed_away = swap(grad_away, "narrow", 2)
    cross_trip = Travel(cross_parcel, *cross_parts, "cross_weights", False)
    tokens_grad = tokens_grad.astype(high)
    ready = self_trip.fold_two(grad_away)
    self_trip.send()
    ready = cross_trip.fold_one(ready)
    gate_sum, up_sum, down_sum, cross_out_sum = feed_trip.end(ready)
    ready = gate_sum
    ready = cross_trip.fold_two(ready)
    cross_trip.send()
    grad_near, landed_away = lax.optimization_barrier((grad_near, landed_away, ready))[:2]
    landed_core = swap(grad_near[local_mem:], "narrow", 1)
    landed_far = swap(landed_away[local_mem:], "narrow", 1)
    self_query_sum, self_key_sum, self_value_sum, cross_query_sum, self_out_sum, gains = (
        self_trip.end(ready)
    )
    memory_grad = land_call(
        mine.reshape(1),
        [after(grad_near, self_query_sum), landed_core, landed_away, landed_far],
    )
    cross_key_sum, cross_value_sum = cross_trip.end(memory_grad)
    gains = gains[: 3 * width // LANES].reshape(3, width)
    return (
        result,
        tokens_grad,
        memory_grad,
        gains[0],
        self_query_sum,
        self_key_sum,
        self_value_sum,
        self_out_sum,
        gains[1],
        cross_query_sum,
        cross_key_sum,
        cross_value_sum,
        cross_out_sum,
        gains[2],
        gate_sum,
        up_sum,
        down_sum,
    )


def solution(mesh):
    in_specs = (
        P("items", "narrow", None),
        P("items", "narrow", None),
        P("items"),
        P("items", "narrow", None),
        P(),
        P(),
        P(),
        P(),
        P(),
        P(),
        P(),
        P(),
        P(),
        P(),
        P(),
        P(),
        P(),
        P(),
    )
    out_specs = (
        P("items", "narrow", None),
        P("items", "narrow", None),
        P("items", "narrow", None),
        P(),
        P("items", "narrow"),
        P("items", "narrow"),
        P("items", "narrow"),
        P("items", "narrow"),
        P(),
        P("items", "narrow"),
        P("items", "narrow"),
        P("items", "narrow"),
        P("items", "narrow"),
        P(),
        P("items", "narrow"),
        P("items", "narrow"),
        P("items", "narrow"),
    )
    return jax.shard_map(body, mesh=mesh, in_specs=in_specs, out_specs=out_specs, check_vma=False)
```

profile of v0, /device:TPU:0, one launch (start us, length us, event | category | flops | bytes accessed | tf_op | source)
XLA Modules:
  0.0 302.7 jit_solution(12888303054536526133)
XLA Ops:
  0.7 2.9 dynamic-slice_bitcast_fusion
  3.6 0.5 collective-permute-start
  4.1 3.9 %all-to-all-start = ((bf16[4,128,768]{2,1,0:T(8,128)(2,1)}), bf16[4,128,768]{2,1,0:T(8,128)(2,1)S(1)}, u32[]{:S(2)}, u32[]{:S(2)}) async-start(bf16[4,128,768]{2,1,0:T(8,128)(2,1)} %param.18), calls=%async_computation | async-start | bytes 1572864 | tf_op jit(solution)/shard_map/all_to_all | solution.py:1161
  8.0 2.2 collective-permute-start.1
  10.4 0.6 dynamic_slice.17
  11.0 1.2 multiply_subtract_fusion.refs_0_
  12.2 0.6 pad_maximum_fusion.gains_ref.refs_4_
  12.8 6.0 %enter_memory_near.1 = (bf16[1024,768]{1,0:T(8,128)(2,1)}, bf16[1024,768]{1,0:T(8,128)(2,1)}, bf16[1024,768]{1,0:T(8,128)(2,1)}) custom-call(bf16[512,768]{1,0:T(8,128)(2,1)} %get-tuple-element.232.first_ref, bf16[512,768]{1,0:T(8,128)(2,1)} %collective-permute-done.second_ref, bf16[768,768]{1,0:T(8,128)(2,1)} %refs_7_.3, bf16[768,768]{1,0:T(8,128)(2,1)} %refs_8_.3), custom_call_target="tpu_custom_call" | custom-call | flops 2300000000 | bytes 1 | tf_op jit(solution)/shard_map/enter_memory_near/pallas_call | solution.py:191
  18.8 1.5 all-to-all-done
  20.3 3.7 %all-to-all-start.1 = ((bf16[4,128,768]{2,1,0:T(8,128)(2,1)}), bf16[4,128,768]{2,1,0:T(8,128)(2,1)S(1)}, u32[]{:S(2)}, u32[]{:S(2)}) async-start(bf16[4,128,768]{2,1,0:T(8,128)(2,1)} %param.21), calls=%async_computation.1 | async-start | bytes 1572864 | tf_op jit(solution)/shard_map/all_to_all | solution.py:1161
  24.0 16.4 %self_forward.1 = (bf16[512,768]{1,0:T(8,128)(2,1)}, bf16[512,768]{1,0:T(8,128)(2,1)}, bf16[512,768]{1,0:T(8,128)(2,1)}, bf16[512,768]{1,0:T(8,128)(2,1)}, bf16[...) custom-call(bf16[512,768]{1,0:T(8,128)(2,1)} %bitcast.30, ...), custom_call_target="tpu_custom_call" | custom-call | flops 9200000000 | bytes 1 | tf_op jit(solution)/shard_map/self_forward/pallas_call | solution.py:150
  40.5 14.9 %cross_forward_near.1 = (bf16[6,1024,1024]{2,1,0:T(8,128)(2,1)}, f32[6,128,1024]{2,1,0:T(8,128)}, f32[6,8,1024]{2,1,0:T(8,128)}) custom-call(s32[4]{0:T(128)} %multiply_subtract_fusion.refs_0_, bf16[512,768]{1,0:T(8,128)(2,1)} %get-tuple-element.117.refs_1_.refs_2_, bf16[1024,768]{1,0:T(8,128)(2,1)} %get-tuple-element.115.refs_2_.refs_3_, ...), custom_call_target="tpu_custom_call" | custom-call | flops 6899999744 | bytes 1 | tf_op jit(solution)/shard_map/cross_forward_near/pallas_call | solution.py:646
  55.4 5.9 %enter_memory_far.1 = (bf16[1024,768]{1,0:T(8,128)(2,1)}, bf16[1024,768]{1,0:T(8,128)(2,1)}, bf16[1024,768]{1,0:T(8,128)(2,1)}) custom-call(bf16[512,768]{1,0:T(8,128)(2,1)} %collective-permute-done.1.first_ref, bf16[512,768]{1,0:T(8,128)(2,1)} %collective-permute-done.2.second_ref, bf16[768,768]{1,0:T(8,128)(2,1)} %refs_7_.3, bf16[768,768]{1,0:T(8,128)(2,1)} %refs_8_.3), custom_call_target="tpu_custom_call" | custom-call | flops 2300000000 | bytes 1 | tf_op jit(solution)/shard_map/enter_memory_far/pallas_call | solution.py:191
  61.3 15.7 %cross_forward_far.1 = (bf16[6,1024,1024]{2,1,0:T(8,128)(2,1)}, bf16[512,768]{1,0:T(8,128)(2,1)}, f32[6,8,1024]{2,1,0:T(8,128)}) custom-call(s32[4]{0:T(128)} %multiply_subtract_fusion.refs_0_, bf16[512,768]{1,0:T(8,128)(2,1)} %get-tuple-element.117.refs_1_.refs_2_, bf16[1024,768]{1,0:T(8,128)(2,1)} %get-tuple-element.121.refs_2_.refs_3_, ...), custom_call_target="tpu_custom_call" | custom-call | flops 6899999744 | bytes 1 | tf_op jit(solution)/shard_map/cross_forward_far/pallas_call | solution.py:646
  77.0 0.9 copy-done.3
  77.9 29.6 %feed_both.1 = (bf16[512,768]{1,0:T(8,128)(2,1)}, f32[512,768]{1,0:T(8,128)}, bf16[512,768]{1,0:T(8,128)(2,1)}, bf16[512,768]{1,0:T(8,128)(2,1)}, f32[1,768]{1,0...) custom-call(s32[1]{0:T(128)} %bitcast.refs_0_, ...), custom_call_target="tpu_custom_call" | custom-call | flops 1150000 | bytes 1 | tf_op jit(solution)/shard_map/feed_both/pallas_call | solution.py:394
  107.5 6.0 %all-to-all-start.2 = ((bf16[4,128,768]{2,1,0:T(8,128)(2,1)}), bf16[4,128,768]{2,1,0:T(8,128)(2,1)S(1)}, u32[]{:S(2)}, u32[]{:S(2)}) async-start(bf16[4,128,768]{2,1,0:T(8,128)(2,1)} %bitcast.36), calls=%async_computation.2 | async-start | bytes 1572864 | tf_op jit(solution)/shard_map/all_to_all | solution.py:1161
  113.6 9.5 %cross_backward_far_a.1 = (f32[512,768]{1,0:T(8,128)}, bf16[1024,768]{1,0:T(8,128)(2,1)}, bf16[1024,768]{1,0:T(8,128)(2,1)}) custom-call(bf16[6,1024,1024]{2,1,0:T(8,128)(2,1)} %get-tuple-element.131.refs_0_, f32[6,8,1024]{2,1,0:T(8,128)} %get-tuple-element.128.refs_1_, bf16[512,768]{1,0:T(8,128)(2,1)} %get-tuple-element.117.refs_1_.refs_2_, ...), custom_call_target="tpu_custom_call" | custom-call | flops 1150000 | bytes 1 | tf_op jit(solution)/shard_map/cross_backward_far_a/pallas_call | solution.py:736
  123.0 2.6 all-to-all-done.2
  125.6 7.7 %feed_weights_one.1 = (bf16[4,1296,128]{2,1,0:T(8,128)(2,1)}, bf16[4,1296,128]{2,1,0:T(8,128)(2,1)}, bf16[4,1296,128]{2,1,0:T(8,128)(2,1)}, bf16[4,1296,128]{2,1,0:T(8,128)(2,1)}) custom-call(s32[1]{0:T(128)} %bitcast.9.mine_ref, bf16[2,4,2592,128]{3,2,1,0:T(8,128)(2,1)} %bitcast.29, bf16[2,4,2592,128]{3,2,1,0:T(8,128)(2,1)} %bitcast.11.received_ref), custom_call_target="tpu_custom_call" | custom-call | flops 1150000 | bytes 1 | tf_op jit(solution)/shard_map/feed_weights_one/pallas_call | solution.py:1019
  133.3 1.9 collective-permute-start.6
  135.2 1.6 collective-permute-start.7
  136.8 9.5 %cross_backward_far_b.1 = (f32[512,768]{1,0:T(8,128)}, bf16[1024,768]{1,0:T(8,128)(2,1)}, bf16[1024,768]{1,0:T(8,128)(2,1)}) custom-call(bf16[6,1024,1024]{2,1,0:T(8,128)(2,1)} %get-tuple-element.131.refs_0_, f32[6,8,1024]{2,1,0:T(8,128)} %get-tuple-element.128.refs_1_, ...), custom_call_target="tpu_custom_call", output_to_operand_aliasing={{0}: (7, {}), {1}: (8, {}), {2}: (9, {})} | custom-call | flops 115000000512 | bytes 1 | tf_op jit(solution)/shard_map/cross_backward_far_b/pallas_call | solution.py:736
  146.3 16.5 %cross_backward_near.1 = (bf16[512,768]{1,0:T(8,128)(2,1)}, bf16[1024,768]{1,0:T(8,128)(2,1)}, bf16[1024,768]{1,0:T(8,128)(2,1)}) custom-call(bf16[6,1024,1024]{2,1,0:T(8,128)(2,1)} %get-tuple-element.127.refs_0_, f32[6,8,1024]{2,1,0:T(8,128)} %get-tuple-element.128.refs_1_, bf16[512,768]{1,0:T(8,128)(2,1)} %get-tuple-element.117.refs_1_.refs_2_, ...), custom_call_target="tpu_custom_call" | custom-call | flops 1150000 | bytes 1 | tf_op jit(solution)/shard_map/cross_backward_near/pallas_call | solution.py:736
  162.8 26.1 %self_backward.1 = (bf16[512,768]{1,0:T(8,128)(2,1)}, bf16[8,1504,128]{2,1,0:T(8,128)(2,1)}, bf16[8,1504,128]{2,1,0:T(8,128)(2,1)}) custom-call(s32[1]{0:T(128)} %bitcast.refs_0_, bf16[512,768]{1,0:T(8,128)(2,1)} %get-tuple-element.143.refs_1_, f32[512,768]{1,0:T(8,128)} %get-tuple-element.125.refs_2_, f32[512,768]{1,0:T(8,128)} %get-tuple-element.144.refs_3_, ...), custom_call_target="tpu_custom_call" | custom-call | flops 1150000 | bytes 1 | tf_op jit(solution)/shard_map/self_backward/pallas_call | solution.py:965
  188.9 3.5 %all-to-all-start.3 = ((bf16[4,128,768]{2,1,0:T(8,128)(2,1)}), bf16[4,128,768]{2,1,0:T(8,128)(2,1)S(1)}, u32[]{:S(2)}, u32[]{:S(2)}) async-start(bf16[4,128,768]{2,1,0:T(8,128)(2,1)} %bitcast.35), calls=%async_computation.3 | async-start | bytes 1572864 | tf_op jit(solution)/shard_map/all_to_all | solution.py:1161
  192.4 0.5 collective-permute-start.4
  192.9 0.7 collective-permute-done.7.refs_3_
  193.6 0.4 copy-done.14
  194.0 0.4 copy-done.15
  194.4 4.2 %feed_weights_two.1 = bf16[4,1296,128]{2,1,0:T(8,128)(2,1)} custom-call(bf16[4,1296,128]{2,1,0:T(8,128)(2,1)} %get-tuple-element.161.refs_0_, bf16[4,1296,128]{2,1,0:T(8,128)(2,1)} %copy-done.14, bf16[4,1296,128]{2,1,0:T(8,128)(2,1)} %copy-done.15, bf16[4,1296,128]{2,1,0:T(8,128)(2,1)} %collective-permute-done.7.refs_3_), custom_call_target="tpu_custom_call" | custom-call | flops 115000000512 | bytes 1 | tf_op jit(solution)/shard_map/feed_weights_two/pallas_call | solution.py:191
  198.7 5.3 %self_weights_one.1 = (bf16[4,752,128]{2,1,0:T(8,128)(2,1)}, bf16[4,752,128]{2,1,0:T(8,128)(2,1)}, bf16[4,752,128]{2,1,0:T(8,128)(2,1)}, bf16[4,752,128]{2,1,0:T(8,128)(2,1)}) custom-call(s32[1]{0:T(128)} %bitcast.9.mine_ref, bf16[2,4,1504,128]{3,2,1,0:T(8,128)(2,1)} %bitcast.33, bf16[2,4,1504,128]{3,2,1,0:T(8,128)(2,1)} %bitcast.15.received_ref), custom_call_target="tpu_custom_call" | custom-call | flops 1150000 | bytes 1 | tf_op jit(solution)/shard_map/self_weights_one/pallas_call | solution.py:1019
  204.1 4.6 %all-to-all-start.4 = ((bf16[4,1296,128]{2,1,0:T(8,128)(2,1)}), bf16[4,1296,128]{2,1,0:T(8,128)(2,1)}, u32[]{:S(2)}, u32[]{:S(2)}) async-start(bf16[4,1296,128]{2,1,0:T(8,128)(2,1)} %feed_weights_two.1), calls=%async_computation.4 | async-start | bytes 2654208 | tf_op jit(solution)/shard_map/all_to_all | solution.py:1136
  208.7 1.7 collective-permute-start.10
  210.4 1.6 collective-permute-start.11
  212.0 0.3 collective-permute-start.12
  212.3 18.4 %memory_back.1 = (bf16[1024,768]{1,0:T(8,128)(2,1)}, bf16[1024,768]{1,0:T(8,128)(2,1)}, bf16[8,576,128]{2,1,0:T(8,128)(2,1)}, bf16[8,576,128]{2,1,0:T(8,128)(2,1)}) custom-call(s32[1]{0:T(128)} %bitcast.refs_0_, bf16[1024,768]{1,0:T(8,128)(2,1)} %get-tuple-element.168.refs_1_, bf16[1024,768]{1,0:T(8,128)(2,1)} %get-tuple-element.169.refs_2_, ...), custom_call_target="tpu_custom_call" | custom-call | flops 115000000512 | bytes 1 | tf_op jit(solution)/shard_map/memory_back/pallas_call | solution.py:494
  230.7 1.7 collective-permute-start.8
  232.5 13.3 %collective-permute-done.11.refs_2_ = bf16[4,752,128]{2,1,0:T(8,128)(2,1)} collective-permute-done((bf16[4,752,128]{2,1,0:T(8,128)(2,1)S(1)}, bf16[4,752,128]{2,1,0:T(8,128)(2,1)}, u32[]{:S(2)}, u32[]{:S(2)}) %collective-permute-start.11) | collective-permute-done | bytes 770080 | tf_op jit(solution)/shard_map/ppermute | solution.py:1101
  245.8 0.9 collective-permute-done.12.refs_3_
  246.7 3.1 %self_weights_two.1 = bf16[4,752,128]{2,1,0:T(8,128)(2,1)} custom-call(bf16[4,752,128]{2,1,0:T(8,128)(2,1)} %get-tuple-element.181.refs_0_, bf16[4,752,128]{2,1,0:T(8,128)(2,1)} %collective-permute-done.10.refs_1_, bf16[4,752,128]{2,1,0:T(8,128)(2,1)} %collective-permute-done.11.refs_2_, bf16[4,752,128]{2,1,0:T(8,128)(2,1)} %collective-permute-done.12.refs_3_), custom_call_target="tpu_custom_call" | custom-call | flops 115000000512 | bytes 1 | tf_op jit(solution)/shard_map/self_weights_two/pallas_call | solution.py:191
  249.8 5.1 %all-to-all-start.5 = ((bf16[4,752,128]{2,1,0:T(8,128)(2,1)}), bf16[4,752,128]{2,1,0:T(8,128)(2,1)}, u32[]{:S(2)}, u32[]{:S(2)}) async-start(bf16[4,752,128]{2,1,0:T(8,128)(2,1)} %self_weights_two.1), calls=%async_computation.5 | async-start | bytes 1540096 | tf_op jit(solution)/shard_map/all_to_all | solution.py:1136
  254.9 3.6 %cross_weights_one.1 = (bf16[2,576,128]{2,1,0:T(8,128)(2,1)}, bf16[2,576,128]{2,1,0:T(8,128)(2,1)}, bf16[2,576,128]{2,1,0:T(8,128)(2,1)}, bf16[2,576,128]{2,1,0:T(8,128)(2,1)}) custom-call(s32[1]{0:T(128)} %bitcast.16.mine_ref, bf16[4,2,576,128]{3,2,1,0:T(8,128)(2,1)} %bitcast.34, bf16[4,2,576,128]{3,2,1,0:T(8,128)(2,1)} %bitcast.18.received_ref), custom_call_target="tpu_custom_call" | custom-call | flops 1150000 | bytes 1 | tf_op jit(solution)/shard_map/cross_weights_one/pallas_call | solution.py:1019
  258.5 2.0 collective-permute-start.13
  260.5 0.8 collective-permute-start.14
  261.3 0.7 collective-permute-start.15
  262.0 1.3 convert_element_type.3
  263.3 2.4 feed_weights_end.1
  265.7 1.7 copy.38
  267.4 8.8 %collective-permute-done.13.refs_1_ = bf16[2,576,128]{2,1,0:T(8,128)(2,1)S(1)} collective-permute-done((bf16[2,576,128]{2,1,0:T(8,128)(2,1)}, bf16[2,576,128]{2,1,0:T(8,128)(2,1)S(1)}, u32[]{:S(2)}, u32[]{:S(2)}) %collective-permute-start.13) | collective-permute-done | bytes 294944 | tf_op jit(solution)/shard_map/ppermute | solution.py:1101
  276.2 5.1 %collective-permute-done.15.refs_3_ = bf16[2,576,128]{2,1,0:T(8,128)(2,1)} collective-permute-done((bf16[2,576,128]{2,1,0:T(8,128)(2,1)}, bf16[2,576,128]{2,1,0:T(8,128)(2,1)}, u32[]{:S(2)}, u32[]{:S(2)}) %collective-permute-start.15) | collective-permute-done | bytes 294944 | tf_op jit(solution)/shard_map/ppermute | solution.py:1101
  281.3 2.1 cross_weights_two.1
  283.5 1.0 slice.22
  284.5 0.3 copy-done.1
  284.8 0.3 collective-permute-start.17
  285.1 4.1 %all-to-all-start.6 = ((bf16[4,288,128]{2,1,0:T(8,128)(2,1)}), bf16[4,288,128]{2,1,0:T(8,128)(2,1)S(1)}, u32[]{:S(2)}, u32[]{:S(2)}) async-start(bf16[4,288,128]{2,1,0:T(8,128)(2,1)} %cross_weights_two.1), calls=%async_computation.6 | async-start | bytes 589824 | tf_op jit(solution)/shard_map/all_to_all | solution.py:1136
  289.2 2.0 self_weights_end.1
  291.2 1.4 slice_bitcast_fusion
  292.6 0.9 copy-done.9
  293.5 4.9 %land_memory.1 = f32[4,512,768]{2,1,0:T(8,128)} custom-call(s32[1]{0:T(128)} %bitcast.13.place_ref, bf16[1024,768]{1,0:T(8,128)(2,1)} %get-tuple-element.200.refs_0_, bf16[512,768]{1,0:T(8,128)(2,1)} %copy-done.9, bf16[1024,768]{1,0:T(8,128)(2,1)} %copy-done.1, bf16[512,768]{1,0:T(8,128)(2,1)} %collective-permute-done.17.refs_3_), custom_call_target="tpu_custom_call" | custom-call | flops 1150000 | bytes 1 | tf_op jit(solution)/shard_map/land_memory/pallas_call | solution.py:521
  298.4 0.8 all-to-all-done.6.refs_0_
  299.2 0.7 copy-done.8
  299.9 1.7 cross_weights_end.1
  301.6 0.9 copy.43
  (58 shorter events, 0.5 us)
Async XLA Ops:
  3.6 6.8 %copy-start.18 = (s32[4]{0:T(128)S(1)}, s32[4]{0:T(128)}, u32[]{:S(2)}) copy-start(s32[4]{0:T(128)} %param.20) | copy-start | bytes 52
  3.6 7.4 %copy-start.11 = (f32[768]{0:T(1024)S(1)}, f32[768]{0:T(1024)}, u32[]{:S(2)}) copy-start(f32[768]{0:T(1024)} %param.32) | copy-start | bytes 9220
  3.6 7.4 %copy-start.12 = (f32[768]{0:T(1024)S(1)}, f32[768]{0:T(1024)}, u32[]{:S(2)}) copy-start(f32[768]{0:T(1024)} %param.27) | copy-start | bytes 9220
  3.6 7.4 %copy-start.13 = (f32[768]{0:T(1024)S(1)}, f32[768]{0:T(1024)}, u32[]{:S(2)}) copy-start(f32[768]{0:T(1024)} %param.22) | copy-start | bytes 9220
  3.6 9.2 %collective-permute-start = (bf16[512,768]{1,0:T(8,128)(2,1)S(1)}, bf16[512,768]{1,0:T(8,128)(2,1)}, u32[]{:S(2)}, u32[]{:S(2)}) collective-permute-start(bf16[512,768]{1,0:T(8,128)(2,1)S(1)} %get-tuple-element.231), channel_id=1, source_target_pairs={{0,1},{1,0},{2,3},{3,2},{4,5},{5,4},{6,7},{7,6},{8,9},{9,8},{10,11... | collective-permute-start | bytes 2359304 | tf_op jit(solution)/shard_map/ppermute | solution.py:765
  4.1 16.2 %all-to-all-start = ((bf16[4,128,768]{2,1,0:T(8,128)(2,1)}), bf16[4,128,768]{2,1,0:T(8,128)(2,1)S(1)}, u32[]{:S(2)}, u32[]{:S(2)}) async-start(bf16[4,128,768]{2,1,0:T(8,128)(2,1)} %param.18), calls=%async_computation | async-start | bytes 1572864 | tf_op jit(solution)/shard_map/all_to_all | solution.py:1161
  8.0 47.4 %collective-permute-start.1 = (bf16[512,768]{1,0:T(8,128)(2,1)S(1)}, bf16[512,768]{1,0:T(8,128)(2,1)}, u32[]{:S(2)}, u32[]{:S(2)}) collective-permute-start(bf16[512,768]{1,0:T(8,128)(2,1)S(1)} %get-tuple-element.233), channel_id=1, source_target_pairs={{0,2},{1,3},{2,0},{3,1},{4,6},{5,7},{6,4},{7,5},{8,10},{9,11},{10,... | collective-permute-start | bytes 2359304 | tf_op jit(solution)/shard_map/ppermute | solution.py:765
  10.2 45.2 %collective-permute-start.2 = (bf16[512,768]{1,0:T(8,128)(2,1)S(1)}, bf16[512,768]{1,0:T(8,128)(2,1)}, u32[]{:S(2)}, u32[]{:S(2)}) collective-permute-start(bf16[512,768]{1,0:T(8,128)(2,1)S(1)} %get-tuple-element.230), channel_id=1, source_target_pairs={{0,3},{1,2},{2,1},{3,0},{4,7},{5,6},{6,5},{7,4},{8,11},{9,10},{10,... | collective-permute-start | bytes 2359304 | tf_op jit(solution)/shard_map/ppermute | solution.py:765
  20.3 3.7 %copy-start.2 = (bf16[4,128,768]{2,1,0:T(8,128)(2,1)}, bf16[4,128,768]{2,1,0:T(8,128)(2,1)S(1)}, u32[]{:S(2)}) copy-start(bf16[4,128,768]{2,1,0:T(8,128)(2,1)S(1)} %all-to-all-done) | copy-start | bytes 2359300
  20.3 56.7 %all-to-all-start.1 = ((bf16[4,128,768]{2,1,0:T(8,128)(2,1)}), bf16[4,128,768]{2,1,0:T(8,128)(2,1)S(1)}, u32[]{:S(2)}, u32[]{:S(2)}) async-start(bf16[4,128,768]{2,1,0:T(8,128)(2,1)} %param.21), calls=%async_computation.1 | async-start | bytes 1572864 | tf_op jit(solution)/shard_map/all_to_all | solution.py:1161
  77.0 0.9 copy-start.3
  107.4 18.2 %collective-permute-start.3 = (bf16[8,2592,128]{2,1,0:T(8,128)(2,1)}, bf16[8,2592,128]{2,1,0:T(8,128)(2,1)}, u32[]{:S(2)}, u32[]{:S(2)}) collective-permute-start(bf16[8,2592,128]{2,1,0:T(8,128)(2,1)} %get-tuple-element.133), channel_id=1, source_target_pairs={{0,1},{1,0},{2,3},{3,2},{4,5},{5,4},{6,7},{7,6},{8,9},{9,8},{10,11... | collective-permute-start | bytes 15925256 | tf_op jit(solution)/shard_map/ppermute | solution.py:765
  107.5 18.1 %all-to-all-start.2 = ((bf16[4,128,768]{2,1,0:T(8,128)(2,1)}), bf16[4,128,768]{2,1,0:T(8,128)(2,1)S(1)}, u32[]{:S(2)}, u32[]{:S(2)}) async-start(bf16[4,128,768]{2,1,0:T(8,128)(2,1)} %bitcast.36), calls=%async_computation.2 | async-start | bytes 1572864 | tf_op jit(solution)/shard_map/all_to_all | solution.py:1161
  125.6 7.7 %copy-start.4 = (bf16[4,128,768]{2,1,0:T(8,128)(2,1)}, bf16[4,128,768]{2,1,0:T(8,128)(2,1)S(1)}, u32[]{:S(2)}) copy-start(bf16[4,128,768]{2,1,0:T(8,128)(2,1)S(1)} %all-to-all-done.2) | copy-start | bytes 2359300
  133.3 59.6 %collective-permute-start.5 = (bf16[4,1296,128]{2,1,0:T(8,128)(2,1)}, bf16[4,1296,128]{2,1,0:T(8,128)(2,1)S(1)}, u32[]{:S(2)}, u32[]{:S(2)}) collective-permute-start(bf16[4,1296,128]{2,1,0:T(8,128)(2,1)} %get-tuple-element.158), channel_id=1, source_target_pairs={{0,2},{1,3},{2,0},{3,1},{4,6},{5,7},{6,4},{7,5},{8,10},{9,11},{10,... | collective-permute-start | bytes 3981320 | tf_op jit(solution)/shard_map/ppermute | solution.py:1101
  133.3 59.6 %collective-permute-start.6 = (bf16[4,1296,128]{2,1,0:T(8,128)(2,1)}, bf16[4,1296,128]{2,1,0:T(8,128)(2,1)S(1)}, u32[]{:S(2)}, u32[]{:S(2)}) collective-permute-start(bf16[4,1296,128]{2,1,0:T(8,128)(2,1)} %get-tuple-element.159), channel_id=1, source_target_pairs={{0,4},{1,5},{2,6},{3,7},{4,0},{5,1},{6,2},{7,3},{8,12},{9,13},{10,... | collective-permute-start | bytes 3981320 | tf_op jit(solution)/shard_map/ppermute | solution.py:1101
  135.2 58.4 %collective-permute-start.7 = (bf16[4,1296,128]{2,1,0:T(8,128)(2,1)}, bf16[4,1296,128]{2,1,0:T(8,128)(2,1)}, u32[]{:S(2)}, u32[]{:S(2)}) collective-permute-start(bf16[4,1296,128]{2,1,0:T(8,128)(2,1)} %get-tuple-element.160), channel_id=1, source_target_pairs={{0,6},{1,7},{2,4},{3,5},{4,2},{5,3},{6,0},{7,1},{8,14},{9,15},{10,... | collective-permute-start | bytes 3981320 | tf_op jit(solution)/shard_map/ppermute | solution.py:1101
  188.9 15.1 %all-to-all-start.3 = ((bf16[4,128,768]{2,1,0:T(8,128)(2,1)}), bf16[4,128,768]{2,1,0:T(8,128)(2,1)S(1)}, u32[]{:S(2)}, u32[]{:S(2)}) async-start(bf16[4,128,768]{2,1,0:T(8,128)(2,1)} %bitcast.35), calls=%async_computation.3 | async-start | bytes 1572864 | tf_op jit(solution)/shard_map/all_to_all | solution.py:1161
  192.4 6.2 %collective-permute-start.4 = (bf16[8,1504,128]{2,1,0:T(8,128)(2,1)}, bf16[8,1504,128]{2,1,0:T(8,128)(2,1)}, u32[]{:S(2)}, u32[]{:S(2)}) collective-permute-start(bf16[8,1504,128]{2,1,0:T(8,128)(2,1)} %get-tuple-element.157), channel_id=1, source_target_pairs={{0,1},{1,0},{2,3},{3,2},{4,5},{5,4},{6,7},{7,6},{8,9},{9,8},{10,11... | collective-permute-start | bytes 9240584 | tf_op jit(solution)/shard_map/ppermute | solution.py:765
  192.9 1.1 copy-start.14
  192.9 1.5 copy-start.15
  204.0 6.4 %copy-start.17 = (bf16[4,752,128]{2,1,0:T(8,128)(2,1)S(1)}, bf16[4,752,128]{2,1,0:T(8,128)(2,1)}, u32[]{:S(2)}) copy-start(bf16[4,752,128]{2,1,0:T(8,128)(2,1)} %get-tuple-element.179) | copy-start | bytes 2310148
  204.0 8.0 %copy-start.16 = (bf16[4,752,128]{2,1,0:T(8,128)(2,1)S(1)}, bf16[4,752,128]{2,1,0:T(8,128)(2,1)}, u32[]{:S(2)}) copy-start(bf16[4,752,128]{2,1,0:T(8,128)(2,1)} %get-tuple-element.180) | copy-start | bytes 2310148
  204.1 26.7 %copy-start.6 = (bf16[4,128,768]{2,1,0:T(8,128)(2,1)}, bf16[4,128,768]{2,1,0:T(8,128)(2,1)S(1)}, u32[]{:S(2)}) copy-start(bf16[4,128,768]{2,1,0:T(8,128)(2,1)S(1)} %all-to-all-done.3) | copy-start | bytes 2359300
  204.1 45.7 %all-to-all-start.4 = ((bf16[4,1296,128]{2,1,0:T(8,128)(2,1)}), bf16[4,1296,128]{2,1,0:T(8,128)(2,1)}, u32[]{:S(2)}, u32[]{:S(2)}) async-start(bf16[4,1296,128]{2,1,0:T(8,128)(2,1)} %feed_weights_two.1), calls=%async_computation.4 | async-start | bytes 2654208 | tf_op jit(solution)/shard_map/all_to_all | solution.py:1136
  208.7 23.7 %collective-permute-start.10 = (bf16[4,752,128]{2,1,0:T(8,128)(2,1)}, bf16[4,752,128]{2,1,0:T(8,128)(2,1)}, u32[]{:S(2)}, u32[]{:S(2)}) collective-permute-start(bf16[4,752,128]{2,1,0:T(8,128)(2,1)} %get-tuple-element.178), channel_id=1, source_target_pairs={{0,2},{1,3},{2,0},{3,1},{4,6},{5,7},{6,4},{7,5},{8,10},{9,11},{10,... | collective-permute-start | bytes 2310152 | tf_op jit(solution)/shard_map/ppermute | solution.py:1101
  210.4 35.3 %collective-permute-start.11 = (bf16[4,752,128]{2,1,0:T(8,128)(2,1)S(1)}, bf16[4,752,128]{2,1,0:T(8,128)(2,1)}, u32[]{:S(2)}, u32[]{:S(2)}) collective-permute-start(bf16[4,752,128]{2,1,0:T(8,128)(2,1)S(1)} %copy-done.17), channel_id=1, source_target_pairs={{0,4},{1,5},{2,6},{3,7},{4,0},{5,1},{6,2},{7,3},{8,12},{9,13},{10,... | collective-permute-start | bytes 2310152 | tf_op jit(solution)/shard_map/ppermute | solution.py:1101
  212.0 34.7 %collective-permute-start.12 = (bf16[4,752,128]{2,1,0:T(8,128)(2,1)S(1)}, bf16[4,752,128]{2,1,0:T(8,128)(2,1)}, u32[]{:S(2)}, u32[]{:S(2)}) collective-permute-start(bf16[4,752,128]{2,1,0:T(8,128)(2,1)S(1)} %copy-done.16), channel_id=1, source_target_pairs={{0,6},{1,7},{2,4},{3,5},{4,2},{5,3},{6,0},{7,1},{8,14},{9,15},{10,... | collective-permute-start | bytes 2310152 | tf_op jit(solution)/shard_map/ppermute | solution.py:1101
  230.7 52.7 %collective-permute-start.8 = (bf16[1024,768]{1,0:T(8,128)(2,1)}, bf16[1024,768]{1,0:T(8,128)(2,1)S(1)}, u32[]{:S(2)}, u32[]{:S(2)}) collective-permute-start(bf16[1024,768]{1,0:T(8,128)(2,1)} %get-tuple-element.175), channel_id=1, source_target_pairs={{0,2},{1,3},{2,0},{3,1},{4,6},{5,7},{6,4},{7,5},{8,10},{9,11},{10,... | collective-permute-start | bytes 4718600 | tf_op jit(solution)/shard_map/ppermute | solution.py:765
  232.5 22.4 %collective-permute-start.9 = (bf16[8,576,128]{2,1,0:T(8,128)(2,1)}, bf16[8,576,128]{2,1,0:T(8,128)(2,1)}, u32[]{:S(2)}, u32[]{:S(2)}) collective-permute-start(bf16[8,576,128]{2,1,0:T(8,128)(2,1)} %get-tuple-element.177), channel_id=1, source_target_pairs={{0,1},{1,0},{2,3},{3,2},{4,5},{5,4},{6,7},{7,6},{8,9},{9,8},{10,11... | collective-permute-start | bytes 3538952 | tf_op jit(solution)/shard_map/ppermute | solution.py:765
  249.8 35.3 %all-to-all-start.5 = ((bf16[4,752,128]{2,1,0:T(8,128)(2,1)}), bf16[4,752,128]{2,1,0:T(8,128)(2,1)}, u32[]{:S(2)}, u32[]{:S(2)}) async-start(bf16[4,752,128]{2,1,0:T(8,128)(2,1)} %self_weights_two.1), calls=%async_computation.5 | async-start | bytes 1540096 | tf_op jit(solution)/shard_map/all_to_all | solution.py:1136
  254.9 7.1 %copy-start.7 = (bf16[4,128,768]{2,1,0:T(8,128)(2,1)S(1)}, bf16[4,128,768]{2,1,0:T(8,128)(2,1)}, u32[]{:S(2)}) copy-start(bf16[4,128,768]{2,1,0:T(8,128)(2,1)} %copy-done.6) | copy-start | bytes 2359300
  258.5 17.7 %collective-permute-start.13 = (bf16[2,576,128]{2,1,0:T(8,128)(2,1)}, bf16[2,576,128]{2,1,0:T(8,128)(2,1)S(1)}, u32[]{:S(2)}, u32[]{:S(2)}) collective-permute-start(bf16[2,576,128]{2,1,0:T(8,128)(2,1)} %get-tuple-element.188), channel_id=1, source_target_pairs={{0,8},{1,9},{2,10},{3,11},{4,12},{5,13},{6,14},{7,15},{8,0},{9,1},... | collective-permute-start | bytes 884744 | tf_op jit(solution)/shard_map/ppermute | solution.py:1101
  260.5 15.7 %collective-permute-start.14 = (bf16[2,576,128]{2,1,0:T(8,128)(2,1)}, bf16[2,576,128]{2,1,0:T(8,128)(2,1)}, u32[]{:S(2)}, u32[]{:S(2)}) collective-permute-start(bf16[2,576,128]{2,1,0:T(8,128)(2,1)} %get-tuple-element.189), channel_id=1, source_target_pairs={{0,4},{1,5},{2,6},{3,7},{4,0},{5,1},{6,2},{7,3},{8,12},{9,13},{10,... | collective-permute-start | bytes 884744 | tf_op jit(solution)/shard_map/ppermute | solution.py:1101
  261.3 20.0 %collective-permute-start.15 = (bf16[2,576,128]{2,1,0:T(8,128)(2,1)}, bf16[2,576,128]{2,1,0:T(8,128)(2,1)}, u32[]{:S(2)}, u32[]{:S(2)}) collective-permute-start(bf16[2,576,128]{2,1,0:T(8,128)(2,1)} %get-tuple-element.190), channel_id=1, source_target_pairs={{0,12},{1,13},{2,14},{3,15},{4,8},{5,9},{6,10},{7,11},{8,4},{9,5},... | collective-permute-start | bytes 884744 | tf_op jit(solution)/shard_map/ppermute | solution.py:1101
  263.3 20.2 %copy-start = (bf16[1024,768]{1,0:T(8,128)(2,1)S(1)}, bf16[1024,768]{1,0:T(8,128)(2,1)}, u32[]{:S(2)}) copy-start(bf16[1024,768]{1,0:T(8,128)(2,1)} %get-tuple-element.200.refs_0_) | copy-start | bytes 4718596
  276.2 5.1 %copy-start.10 = (bf16[2,576,128]{2,1,0:T(8,128)(2,1)}, bf16[2,576,128]{2,1,0:T(8,128)(2,1)S(1)}, u32[]{:S(2)}) copy-start(bf16[2,576,128]{2,1,0:T(8,128)(2,1)S(1)} %collective-permute-done.13.refs_1_) | copy-start | bytes 884740
  283.4 1.4 copy-start.1
  284.5 8.1 %collective-permute-start.16 = (bf16[512,768]{1,0:T(8,128)(2,1)}, bf16[512,768]{1,0:T(8,128)(2,1)S(1)}, u32[]{:S(2)}, u32[]{:S(2)}) collective-permute-start(bf16[512,768]{1,0:T(8,128)(2,1)} %slice.22), channel_id=1, source_target_pairs={{0,1},{1,0},{2,3},{3,2},{4,5},{5,4},{6,7},{7,6},{8,9},{9,8},{10,11... | collective-permute-start | bytes 2359304 | tf_op jit(solution)/shard_map/ppermute | solution.py:765
  284.8 7.7 %collective-permute-start.17 = (bf16[512,768]{1,0:T(8,128)(2,1)S(1)}, bf16[512,768]{1,0:T(8,128)(2,1)}, u32[]{:S(2)}, u32[]{:S(2)}) collective-permute-start(bf16[512,768]{1,0:T(8,128)(2,1)S(1)} %slice.23), channel_id=1, source_target_pairs={{0,1},{1,0},{2,3},{3,2},{4,5},{5,4},{6,7},{7,6},{8,9},{9,8},{10,11... | collective-permute-start | bytes 2359304 | tf_op jit(solution)/shard_map/ppermute | solution.py:765
  285.1 14.1 %all-to-all-start.6 = ((bf16[4,288,128]{2,1,0:T(8,128)(2,1)}), bf16[4,288,128]{2,1,0:T(8,128)(2,1)S(1)}, u32[]{:S(2)}, u32[]{:S(2)}) async-start(bf16[4,288,128]{2,1,0:T(8,128)(2,1)} %cross_weights_two.1), calls=%async_computation.6 | async-start | bytes 589824 | tf_op jit(solution)/shard_map/all_to_all | solution.py:1136
  292.6 0.9 copy-start.9
  293.5 8.1 %copy-start.5 = (bf16[4,128,768]{2,1,0:T(8,128)(2,1)S(1)}, bf16[4,128,768]{2,1,0:T(8,128)(2,1)}, u32[]{:S(2)}) copy-start(bf16[4,128,768]{2,1,0:T(8,128)(2,1)} %copy-done.4) | copy-start | bytes 2359300
  299.2 0.7 copy-start.8
where the time goes:
time: 307 us; the launch traced here: 303 us
  Pallas kernels  206 us (67%)
  starting transfers between devices  46.9 us (15%)
  waiting for transfers between devices  33.7 us (11%)
  local copies, waits for them, and re-layouts  12.2 us (4%)
    pallas_call x3, Pallas kernels, attend_backward(): pl.pallas_call(lambda *refs: attend_backward_kernel(chunks, offset, len(b...  35.5 us
    pallas_call x2, Pallas kernels, attend_forward(): pl.pallas_call(lambda *refs: attend_forward_kernel(causal, chunks, len(be...  30.5 us
    pallas_call x1, Pallas kernels, feed_call(): pl.pallas_call(lambda *refs: feed_both(parcel, parts, *refs), grid=(parts...  29.6 us
    ppermute x9, waiting for transfers between devices, fold_one(): lax.ppermute(part, ('items', 'narrow'), self.joint(*partner))  28.8 us
    pallas_call x8, Pallas kernels, one_step_call(): pl.pallas_call(kernel, in_specs=[smem if piece.dtype == jnp.int32 else vm...  27.5 us
    pallas_call x1, Pallas kernels, self_backward_call(): pl.pallas_call(lambda *refs: self_backward(parcel, *refs), grid=(pairs,),...  26.1 us
    pallas_call x1, Pallas kernels, memory_back_call(): pl.pallas_call(lambda *refs: memory_back(parcel, *refs), grid=(4,), in_sp...  18.4 us
    all_to_all x4, starting transfers between devices, exchange(): lax.all_to_all(piece, 'narrow', split_axis=0, concat_axis=0, tiled=True)  17.1 us
  transfers between devices with their start and end apart: 25, of which 9 were waited for; matrix products, arithmetic and copies ran while one was open for 3% of the time, Pallas kernels for 55%

commit v1 on v0

--- a/solution.py
+++ b/solution.py
@@ -253,13 +253,13 @@
     sum_ref,
     back_ref,
     sides_ref,
-    kept_ref,
-    sent_ref,
+    both_ref,
     done_ref,
 ):
     step = pl.program_id(0)
     core = core_ref[0]
     gain = gain_ref[2:3, :]
+    kept_ref, sent_ref = both_ref.at[0], both_ref.at[1]
 
     @pl.when(step == 0)
     def _():
@@ -312,23 +312,24 @@
     sum_ref[...] = output
     back_ref[...] = back_sum
     side = (step >> 1) * parcel.own
+    other = (step & 1) ^ core
+    for job in (0, 1):
+        rows = parcel.heights[job]
+        for which, pair in enumerate(grads):
+            product = plain_dot(turned, pair[job]).astype(low)
+            for tile in range(size // LANES):
+                at = side + parcel.at[job] + (which * size // LANES + tile) * rows
+                at = pl.multiple_of(at, 16)
+                for block in range(BLOCKS):
+                    both_ref[other, place(block), pl.ds(at, rows), :] = product[
+                        block * rows : (block + 1) * rows, tile * LANES : (tile + 1) * LANES
+                    ]
     for kind, (side_ref, target_ref) in enumerate(
         ((kept_ref, kept_out_ref), (sent_ref, sent_out_ref))
     ):
 
-        @pl.when(((step & 1) ^ core) == kind)
+        @pl.when(other == kind)
         def _():
-            for job in (0, 1):
-                rows = parcel.heights[job]
-                for which, pair in enumerate(grads):
-                    product = plain_dot(turned, pair[job]).astype(low)
-                    for tile in range(size // LANES):
-                        at = side + parcel.at[job] + (which * size // LANES + tile) * rows
-                        at = pl.multiple_of(at, 16)
-                        for block in range(BLOCKS):
-                            side_ref[place(block), pl.ds(at, rows), :] = product[
-                                block * rows : (block + 1) * rows, tile * LANES : (tile + 1) * LANES
-                            ]
             copies(side_ref, target_ref, pl.multiple_of(side, 16), inner, step).start()
 
     rows = parcel.heights[2]
@@ -417,8 +418,7 @@
             pltpu.VMEM((tokens, width), high),
             pltpu.VMEM((tokens, width), high),
             pltpu.VMEM((tokens, width), low),
-            pltpu.VMEM(parcel_shape, low),
-            pltpu.VMEM(parcel_shape, low),
+            pltpu.VMEM((2, *parcel_shape), low),
             pltpu.SemaphoreType.DMA((parts + 4,)),
         ],
         cost_estimate=cost("feed_both"),

time: 307 us -> 302 us (0.984)
  Pallas kernels: 206 us -> 202 us
where the time goes in v1:
time: 302 us; the launch traced here: 297 us
  Pallas kernels  202 us (67%)
  starting transfers between devices  47.2 us (16%)
  waiting for transfers between devices  32.4 us (11%)
  local copies, waits for them, and re-layouts  11.7 us (4%)
  other arithmetic  3.04 us (1%)
    pallas_call x3, Pallas kernels, attend_backward(): pl.pallas_call(lambda *refs: attend_backward_kernel(chunks, offset, len(b...  35.5 us
    pallas_call x2, Pallas kernels, attend_forward(): pl.pallas_call(lambda *refs: attend_forward_kernel(causal, chunks, len(be...  28.3 us
    ppermute x9, waiting for transfers between devices, fold_one(): lax.ppermute(part, ('items', 'narrow'), self.joint(*partner))  28 us
    pallas_call x1, Pallas kernels, feed_call(): pl.pallas_call(lambda *refs: feed_both(parcel, parts, *refs), grid=(parts...  27.9 us
    pallas_call x8, Pallas kernels, one_step_call(): pl.pallas_call(kernel, in_specs=[smem if piece.dtype == jnp.int32 else vm...  27.5 us
    pallas_call x1, Pallas kernels, self_backward_call(): pl.pallas_call(lambda *refs: self_backward(parcel, *refs), grid=(pairs,),...  26.1 us
    pallas_call x1, Pallas kernels, memory_back_call(): pl.pallas_call(lambda *refs: memory_back(parcel, *refs), grid=(4,), in_sp...  18.4 us
    pallas_call x3, Pallas kernels, fold_one_call(): pl.pallas_call(fold_one, grid_spec=pltpu.PrefetchScalarGridSpec(num_scala...  16.7 us
  transfers between devices with their start and end apart: 25, of which 9 were waited for; matrix products, arithmetic and copies ran while one was open for 3% of the time, Pallas kernels for 55%

profile of v1, /device:TPU:0, one launch (start us, length us, event | category | flops | bytes accessed | tf_op | source)
XLA Modules:
  0.0 297.2 jit_solution(8346862187698168370)
XLA Ops:
  0.7 2.9 dynamic-slice_bitcast_fusion
  3.6 0.5 collective-permute-start
  4.1 3.9 %all-to-all-start = ((bf16[4,128,768]{2,1,0:T(8,128)(2,1)}), bf16[4,128,768]{2,1,0:T(8,128)(2,1)S(1)}, u32[]{:S(2)}, u32[]{:S(2)}) async-start(bf16[4,128,768]{2,1,0:T(8,128)(2,1)} %param.18), calls=%async_computation | async-start | bytes 1572864 | tf_op jit(solution)/shard_map/all_to_all | solution.py:1161
  8.0 2.2 collective-permute-start.1
  10.4 0.6 dynamic_slice.17
  11.0 1.2 multiply_subtract_fusion.refs_0_
  12.2 0.6 pad_maximum_fusion.gains_ref.refs_4_
  12.8 6.0 %enter_memory_near.1 = (bf16[1024,768]{1,0:T(8,128)(2,1)}, bf16[1024,768]{1,0:T(8,128)(2,1)}, bf16[1024,768]{1,0:T(8,128)(2,1)}) custom-call(bf16[512,768]{1,0:T(8,128)(2,1)} %get-tuple-element.232.first_ref, bf16[512,768]{1,0:T(8,128)(2,1)} %collective-permute-done.second_ref, bf16[768,768]{1,0:T(8,128)(2,1)} %refs_7_.3, bf16[768,768]{1,0:T(8,128)(2,1)} %refs_8_.3), custom_call_target="tpu_custom_call" | custom-call | flops 2300000000 | bytes 1 | tf_op jit(solution)/shard_map/enter_memory_near/pallas_call | solution.py:191
  18.8 1.5 all-to-all-done
  20.3 3.7 %all-to-all-start.1 = ((bf16[4,128,768]{2,1,0:T(8,128)(2,1)}), bf16[4,128,768]{2,1,0:T(8,128)(2,1)S(1)}, u32[]{:S(2)}, u32[]{:S(2)}) async-start(bf16[4,128,768]{2,1,0:T(8,128)(2,1)} %param.21), calls=%async_computation.1 | async-start | bytes 1572864 | tf_op jit(solution)/shard_map/all_to_all | solution.py:1161
  24.0 16.4 %self_forward.1 = (bf16[512,768]{1,0:T(8,128)(2,1)}, bf16[512,768]{1,0:T(8,128)(2,1)}, bf16[512,768]{1,0:T(8,128)(2,1)}, bf16[512,768]{1,0:T(8,128)(2,1)}, bf16[...) custom-call(bf16[512,768]{1,0:T(8,128)(2,1)} %bitcast.30, ...), custom_call_target="tpu_custom_call" | custom-call | flops 9200000000 | bytes 1 | tf_op jit(solution)/shard_map/self_forward/pallas_call | solution.py:150
  40.5 13.8 %cross_forward_near.1 = (bf16[6,1024,1024]{2,1,0:T(8,128)(2,1)}, f32[6,128,1024]{2,1,0:T(8,128)}, f32[6,8,1024]{2,1,0:T(8,128)}) custom-call(s32[4]{0:T(128)} %multiply_subtract_fusion.refs_0_, bf16[512,768]{1,0:T(8,128)(2,1)} %get-tuple-element.117.refs_1_.refs_2_, bf16[1024,768]{1,0:T(8,128)(2,1)} %get-tuple-element.115.refs_2_.refs_3_, ...), custom_call_target="tpu_custom_call" | custom-call | flops 6899999744 | bytes 1 | tf_op jit(solution)/shard_map/cross_forward_near/pallas_call | solution.py:646
  54.3 5.9 %enter_memory_far.1 = (bf16[1024,768]{1,0:T(8,128)(2,1)}, bf16[1024,768]{1,0:T(8,128)(2,1)}, bf16[1024,768]{1,0:T(8,128)(2,1)}) custom-call(bf16[512,768]{1,0:T(8,128)(2,1)} %collective-permute-done.1.first_ref, bf16[512,768]{1,0:T(8,128)(2,1)} %collective-permute-done.2.second_ref, bf16[768,768]{1,0:T(8,128)(2,1)} %refs_7_.3, bf16[768,768]{1,0:T(8,128)(2,1)} %refs_8_.3), custom_call_target="tpu_custom_call" | custom-call | flops 2300000000 | bytes 1 | tf_op jit(solution)/shard_map/enter_memory_far/pallas_call | solution.py:191
  60.2 14.6 %cross_forward_far.1 = (bf16[6,1024,1024]{2,1,0:T(8,128)(2,1)}, bf16[512,768]{1,0:T(8,128)(2,1)}, f32[6,8,1024]{2,1,0:T(8,128)}) custom-call(s32[4]{0:T(128)} %multiply_subtract_fusion.refs_0_, bf16[512,768]{1,0:T(8,128)(2,1)} %get-tuple-element.117.refs_1_.refs_2_, bf16[1024,768]{1,0:T(8,128)(2,1)} %get-tuple-element.121.refs_2_.refs_3_, ...), custom_call_target="tpu_custom_call" | custom-call | flops 6899999744 | bytes 1 | tf_op jit(solution)/shard_map/cross_forward_far/pallas_call | solution.py:646
  74.8 0.9 copy-done.3
  75.6 27.9 %feed_both.1 = (bf16[512,768]{1,0:T(8,128)(2,1)}, f32[512,768]{1,0:T(8,128)}, bf16[512,768]{1,0:T(8,128)(2,1)}, bf16[512,768]{1,0:T(8,128)(2,1)}, f32[1,768]{1,0...) custom-call(s32[1]{0:T(128)} %bitcast.refs_0_, ...), custom_call_target="tpu_custom_call" | custom-call | flops 1150000 | bytes 1 | tf_op jit(solution)/shard_map/feed_both/pallas_call | solution.py:395
  103.6 0.6 collective-permute-start.3
  104.1 4.0 %all-to-all-start.2 = ((bf16[4,128,768]{2,1,0:T(8,128)(2,1)}), bf16[4,128,768]{2,1,0:T(8,128)(2,1)S(1)}, u32[]{:S(2)}, u32[]{:S(2)}) async-start(bf16[4,128,768]{2,1,0:T(8,128)(2,1)} %bitcast.36), calls=%async_computation.2 | async-start | bytes 1572864 | tf_op jit(solution)/shard_map/all_to_all | solution.py:1161
  108.1 9.5 %cross_backward_far_a.1 = (f32[512,768]{1,0:T(8,128)}, bf16[1024,768]{1,0:T(8,128)(2,1)}, bf16[1024,768]{1,0:T(8,128)(2,1)}) custom-call(bf16[6,1024,1024]{2,1,0:T(8,128)(2,1)} %get-tuple-element.131.refs_0_, f32[6,8,1024]{2,1,0:T(8,128)} %get-tuple-element.128.refs_1_, bf16[512,768]{1,0:T(8,128)(2,1)} %get-tuple-element.117.refs_1_.refs_2_, ...), custom_call_target="tpu_custom_call" | custom-call | flops 1150000 | bytes 1 | tf_op jit(solution)/shard_map/cross_backward_far_a/pallas_call | solution.py:736
  117.6 2.1 all-to-all-done.2
  119.7 7.7 %feed_weights_one.1 = (bf16[4,1296,128]{2,1,0:T(8,128)(2,1)}, bf16[4,1296,128]{2,1,0:T(8,128)(2,1)}, bf16[4,1296,128]{2,1,0:T(8,128)(2,1)}, bf16[4,1296,128]{2,1,0:T(8,128)(2,1)}) custom-call(s32[1]{0:T(128)} %bitcast.9.mine_ref, bf16[2,4,2592,128]{3,2,1,0:T(8,128)(2,1)} %bitcast.29, bf16[2,4,2592,128]{3,2,1,0:T(8,128)(2,1)} %bitcast.11.received_ref), custom_call_target="tpu_custom_call" | custom-call | flops 1150000 | bytes 1 | tf_op jit(solution)/shard_map/feed_weights_one/pallas_call | solution.py:1019
  127.4 0.4 collective-permute-start.5
  127.8 2.0 collective-permute-start.6
  129.7 1.2 collective-permute-start.7
  130.9 9.5 %cross_backward_far_b.1 = (f32[512,768]{1,0:T(8,128)}, bf16[1024,768]{1,0:T(8,128)(2,1)}, bf16[1024,768]{1,0:T(8,128)(2,1)}) custom-call(bf16[6,1024,1024]{2,1,0:T(8,128)(2,1)} %get-tuple-element.131.refs_0_, f32[6,8,1024]{2,1,0:T(8,128)} %get-tuple-element.128.refs_1_, ...), custom_call_target="tpu_custom_call", output_to_operand_aliasing={{0}: (7, {}), {1}: (8, {}), {2}: (9, {})} | custom-call | flops 115000000512 | bytes 1 | tf_op jit(solution)/shard_map/cross_backward_far_b/pallas_call | solution.py:736
  140.4 16.5 %cross_backward_near.1 = (bf16[512,768]{1,0:T(8,128)(2,1)}, bf16[1024,768]{1,0:T(8,128)(2,1)}, bf16[1024,768]{1,0:T(8,128)(2,1)}) custom-call(bf16[6,1024,1024]{2,1,0:T(8,128)(2,1)} %get-tuple-element.127.refs_0_, f32[6,8,1024]{2,1,0:T(8,128)} %get-tuple-element.128.refs_1_, bf16[512,768]{1,0:T(8,128)(2,1)} %get-tuple-element.117.refs_1_.refs_2_, ...), custom_call_target="tpu_custom_call" | custom-call | flops 1150000 | bytes 1 | tf_op jit(solution)/shard_map/cross_backward_near/pallas_call | solution.py:736
  156.9 26.1 %self_backward.1 = (bf16[512,768]{1,0:T(8,128)(2,1)}, bf16[8,1504,128]{2,1,0:T(8,128)(2,1)}, bf16[8,1504,128]{2,1,0:T(8,128)(2,1)}) custom-call(s32[1]{0:T(128)} %bitcast.refs_0_, bf16[512,768]{1,0:T(8,128)(2,1)} %get-tuple-element.143.refs_1_, f32[512,768]{1,0:T(8,128)} %get-tuple-element.125.refs_2_, f32[512,768]{1,0:T(8,128)} %get-tuple-element.144.refs_3_, ...), custom_call_target="tpu_custom_call" | custom-call | flops 1150000 | bytes 1 | tf_op jit(solution)/shard_map/self_backward/pallas_call | solution.py:965
  183.0 3.5 %all-to-all-start.3 = ((bf16[4,128,768]{2,1,0:T(8,128)(2,1)}), bf16[4,128,768]{2,1,0:T(8,128)(2,1)S(1)}, u32[]{:S(2)}, u32[]{:S(2)}) async-start(bf16[4,128,768]{2,1,0:T(8,128)(2,1)} %bitcast.35), calls=%async_computation.3 | async-start | bytes 1572864 | tf_op jit(solution)/shard_map/all_to_all | solution.py:1161
  186.5 0.5 collective-permute-start.4
  187.0 1.2 collective-permute-done.7.refs_3_
  188.5 4.2 %feed_weights_two.1 = bf16[4,1296,128]{2,1,0:T(8,128)(2,1)} custom-call(bf16[4,1296,128]{2,1,0:T(8,128)(2,1)} %get-tuple-element.161.refs_0_, bf16[4,1296,128]{2,1,0:T(8,128)(2,1)} %copy-done.14, bf16[4,1296,128]{2,1,0:T(8,128)(2,1)} %copy-done.15, bf16[4,1296,128]{2,1,0:T(8,128)(2,1)} %collective-permute-done.7.refs_3_), custom_call_target="tpu_custom_call" | custom-call | flops 115000000512 | bytes 1 | tf_op jit(solution)/shard_map/feed_weights_two/pallas_call | solution.py:191
  192.7 5.3 %self_weights_one.1 = (bf16[4,752,128]{2,1,0:T(8,128)(2,1)}, bf16[4,752,128]{2,1,0:T(8,128)(2,1)}, bf16[4,752,128]{2,1,0:T(8,128)(2,1)}, bf16[4,752,128]{2,1,0:T(8,128)(2,1)}) custom-call(s32[1]{0:T(128)} %bitcast.9.mine_ref, bf16[2,4,1504,128]{3,2,1,0:T(8,128)(2,1)} %bitcast.33, bf16[2,4,1504,128]{3,2,1,0:T(8,128)(2,1)} %bitcast.15.received_ref), custom_call_target="tpu_custom_call" | custom-call | flops 1150000 | bytes 1 | tf_op jit(solution)/shard_map/self_weights_one/pallas_call | solution.py:1019
  198.1 5.7 %all-to-all-start.4 = ((bf16[4,1296,128]{2,1,0:T(8,128)(2,1)}), bf16[4,1296,128]{2,1,0:T(8,128)(2,1)}, u32[]{:S(2)}, u32[]{:S(2)}) async-start(bf16[4,1296,128]{2,1,0:T(8,128)(2,1)} %feed_weights_two.1), calls=%async_computation.4 | async-start | bytes 2654208 | tf_op jit(solution)/shard_map/all_to_all | solution.py:1136
  203.8 1.7 collective-permute-start.10
  205.5 1.5 collective-permute-start.11
  207.0 0.3 collective-permute-start.12
  207.4 18.4 %memory_back.1 = (bf16[1024,768]{1,0:T(8,128)(2,1)}, bf16[1024,768]{1,0:T(8,128)(2,1)}, bf16[8,576,128]{2,1,0:T(8,128)(2,1)}, bf16[8,576,128]{2,1,0:T(8,128)(2,1)}) custom-call(s32[1]{0:T(128)} %bitcast.refs_0_, bf16[1024,768]{1,0:T(8,128)(2,1)} %get-tuple-element.168.refs_1_, bf16[1024,768]{1,0:T(8,128)(2,1)} %get-tuple-element.169.refs_2_, ...), custom_call_target="tpu_custom_call" | custom-call | flops 115000000512 | bytes 1 | tf_op jit(solution)/shard_map/memory_back/pallas_call | solution.py:494
  225.8 1.7 collective-permute-start.8
  227.5 12.7 %collective-permute-done.11.refs_2_ = bf16[4,752,128]{2,1,0:T(8,128)(2,1)} collective-permute-done((bf16[4,752,128]{2,1,0:T(8,128)(2,1)S(1)}, bf16[4,752,128]{2,1,0:T(8,128)(2,1)}, u32[]{:S(2)}, u32[]{:S(2)}) %collective-permute-start.11) | collective-permute-done | bytes 770080 | tf_op jit(solution)/shard_map/ppermute | solution.py:1101
  240.3 1.5 collective-permute-done.12.refs_3_
  241.7 3.1 %self_weights_two.1 = bf16[4,752,128]{2,1,0:T(8,128)(2,1)} custom-call(bf16[4,752,128]{2,1,0:T(8,128)(2,1)} %get-tuple-element.181.refs_0_, bf16[4,752,128]{2,1,0:T(8,128)(2,1)} %collective-permute-done.10.refs_1_, bf16[4,752,128]{2,1,0:T(8,128)(2,1)} %collective-permute-done.11.refs_2_, bf16[4,752,128]{2,1,0:T(8,128)(2,1)} %collective-permute-done.12.refs_3_), custom_call_target="tpu_custom_call" | custom-call | flops 115000000512 | bytes 1 | tf_op jit(solution)/shard_map/self_weights_two/pallas_call | solution.py:191
  244.8 5.1 %all-to-all-start.5 = ((bf16[4,752,128]{2,1,0:T(8,128)(2,1)}), bf16[4,752,128]{2,1,0:T(8,128)(2,1)}, u32[]{:S(2)}, u32[]{:S(2)}) async-start(bf16[4,752,128]{2,1,0:T(8,128)(2,1)} %self_weights_two.1), calls=%async_computation.5 | async-start | bytes 1540096 | tf_op jit(solution)/shard_map/all_to_all | solution.py:1136
  250.0 3.6 %cross_weights_one.1 = (bf16[2,576,128]{2,1,0:T(8,128)(2,1)}, bf16[2,576,128]{2,1,0:T(8,128)(2,1)}, bf16[2,576,128]{2,1,0:T(8,128)(2,1)}, bf16[2,576,128]{2,1,0:T(8,128)(2,1)}) custom-call(s32[1]{0:T(128)} %bitcast.16.mine_ref, bf16[4,2,576,128]{3,2,1,0:T(8,128)(2,1)} %bitcast.34, bf16[4,2,576,128]{3,2,1,0:T(8,128)(2,1)} %bitcast.18.received_ref), custom_call_target="tpu_custom_call" | custom-call | flops 1150000 | bytes 1 | tf_op jit(solution)/shard_map/cross_weights_one/pallas_call | solution.py:1019
  253.6 2.0 collective-permute-start.13
  255.6 0.5 collective-permute-start.14
  256.1 1.0 collective-permute-start.15
  257.1 1.3 convert_element_type.3
  258.4 2.4 feed_weights_end.1
  260.8 1.7 copy.38
  262.5 8.2 %collective-permute-done.13.refs_1_ = bf16[2,576,128]{2,1,0:T(8,128)(2,1)S(1)} collective-permute-done((bf16[2,576,128]{2,1,0:T(8,128)(2,1)}, bf16[2,576,128]{2,1,0:T(8,128)(2,1)S(1)}, u32[]{:S(2)}, u32[]{:S(2)}) %collective-permute-start.13) | collective-permute-done | bytes 294944 | tf_op jit(solution)/shard_map/ppermute | solution.py:1101
  270.7 4.4 %collective-permute-done.15.refs_3_ = bf16[2,576,128]{2,1,0:T(8,128)(2,1)} collective-permute-done((bf16[2,576,128]{2,1,0:T(8,128)(2,1)}, bf16[2,576,128]{2,1,0:T(8,128)(2,1)}, u32[]{:S(2)}, u32[]{:S(2)}) %collective-permute-start.15) | collective-permute-done | bytes 294944 | tf_op jit(solution)/shard_map/ppermute | solution.py:1101
  275.1 2.1 cross_weights_two.1
  277.2 1.0 slice.22
  278.2 0.3 copy-done.1
  278.6 0.3 collective-permute-start.17
  278.8 4.9 %all-to-all-start.6 = ((bf16[4,288,128]{2,1,0:T(8,128)(2,1)}), bf16[4,288,128]{2,1,0:T(8,128)(2,1)S(1)}, u32[]{:S(2)}, u32[]{:S(2)}) async-start(bf16[4,288,128]{2,1,0:T(8,128)(2,1)} %cross_weights_two.1), calls=%async_computation.6 | async-start | bytes 589824 | tf_op jit(solution)/shard_map/all_to_all | solution.py:1136
  283.7 2.0 self_weights_end.1
  285.7 1.4 slice_bitcast_fusion
  287.1 0.9 copy-done.9
  288.0 4.9 %land_memory.1 = f32[4,512,768]{2,1,0:T(8,128)} custom-call(s32[1]{0:T(128)} %bitcast.13.place_ref, bf16[1024,768]{1,0:T(8,128)(2,1)} %get-tuple-element.200.refs_0_, bf16[512,768]{1,0:T(8,128)(2,1)} %copy-done.9, bf16[1024,768]{1,0:T(8,128)(2,1)} %copy-done.1, bf16[512,768]{1,0:T(8,128)(2,1)} %collective-permute-done.17.refs_3_), custom_call_target="tpu_custom_call" | custom-call | flops 1150000 | bytes 1 | tf_op jit(solution)/shard_map/land_memory/pallas_call | solution.py:521
  292.9 0.8 all-to-all-done.6.refs_0_
  293.7 0.7 copy-done.8
  294.4 1.7 cross_weights_end.1
  296.1 0.9 copy.43
  (58 shorter events, 0.7 us)
Async XLA Ops:
  3.6 6.8 %copy-start.18 = (s32[4]{0:T(128)S(1)}, s32[4]{0:T(128)}, u32[]{:S(2)}) copy-start(s32[4]{0:T(128)} %param.20) | copy-start | bytes 52
  3.6 7.4 %copy-start.11 = (f32[768]{0:T(1024)S(1)}, f32[768]{0:T(1024)}, u32[]{:S(2)}) copy-start(f32[768]{0:T(1024)} %param.32) | copy-start | bytes 9220
  3.6 7.4 %copy-start.12 = (f32[768]{0:T(1024)S(1)}, f32[768]{0:T(1024)}, u32[]{:S(2)}) copy-start(f32[768]{0:T(1024)} %param.27) | copy-start | bytes 9220
  3.6 7.4 %copy-start.13 = (f32[768]{0:T(1024)S(1)}, f32[768]{0:T(1024)}, u32[]{:S(2)}) copy-start(f32[768]{0:T(1024)} %param.22) | copy-start | bytes 9220
  3.6 9.2 %collective-permute-start = (bf16[512,768]{1,0:T(8,128)(2,1)S(1)}, bf16[512,768]{1,0:T(8,128)(2,1)}, u32[]{:S(2)}, u32[]{:S(2)}) collective-permute-start(bf16[512,768]{1,0:T(8,128)(2,1)S(1)} %get-tuple-element.231), channel_id=1, source_target_pairs={{0,1},{1,0},{2,3},{3,2},{4,5},{5,4},{6,7},{7,6},{8,9},{9,8},{10,11... | collective-permute-start | bytes 2359304 | tf_op jit(solution)/shard_map/ppermute | solution.py:765
  4.1 16.2 %all-to-all-start = ((bf16[4,128,768]{2,1,0:T(8,128)(2,1)}), bf16[4,128,768]{2,1,0:T(8,128)(2,1)S(1)}, u32[]{:S(2)}, u32[]{:S(2)}) async-start(bf16[4,128,768]{2,1,0:T(8,128)(2,1)} %param.18), calls=%async_computation | async-start | bytes 1572864 | tf_op jit(solution)/shard_map/all_to_all | solution.py:1161
  8.0 46.3 %collective-permute-start.1 = (bf16[512,768]{1,0:T(8,128)(2,1)S(1)}, bf16[512,768]{1,0:T(8,128)(2,1)}, u32[]{:S(2)}, u32[]{:S(2)}) collective-permute-start(bf16[512,768]{1,0:T(8,128)(2,1)S(1)} %get-tuple-element.233), channel_id=1, source_target_pairs={{0,2},{1,3},{2,0},{3,1},{4,6},{5,7},{6,4},{7,5},{8,10},{9,11},{10,... | collective-permute-start | bytes 2359304 | tf_op jit(solution)/shard_map/ppermute | solution.py:765
  10.2 44.1 %collective-permute-start.2 = (bf16[512,768]{1,0:T(8,128)(2,1)S(1)}, bf16[512,768]{1,0:T(8,128)(2,1)}, u32[]{:S(2)}, u32[]{:S(2)}) collective-permute-start(bf16[512,768]{1,0:T(8,128)(2,1)S(1)} %get-tuple-element.230), channel_id=1, source_target_pairs={{0,3},{1,2},{2,1},{3,0},{4,7},{5,6},{6,5},{7,4},{8,11},{9,10},{10,... | collective-permute-start | bytes 2359304 | tf_op jit(solution)/shard_map/ppermute | solution.py:765
  20.3 3.7 %copy-start.2 = (bf16[4,128,768]{2,1,0:T(8,128)(2,1)}, bf16[4,128,768]{2,1,0:T(8,128)(2,1)S(1)}, u32[]{:S(2)}) copy-start(bf16[4,128,768]{2,1,0:T(8,128)(2,1)S(1)} %all-to-all-done) | copy-start | bytes 2359300
  20.3 54.5 %all-to-all-start.1 = ((bf16[4,128,768]{2,1,0:T(8,128)(2,1)}), bf16[4,128,768]{2,1,0:T(8,128)(2,1)S(1)}, u32[]{:S(2)}, u32[]{:S(2)}) async-start(bf16[4,128,768]{2,1,0:T(8,128)(2,1)} %param.21), calls=%async_computation.1 | async-start | bytes 1572864 | tf_op jit(solution)/shard_map/all_to_all | solution.py:1161
  74.8 0.9 copy-start.3
  103.6 16.1 %collective-permute-start.3 = (bf16[8,2592,128]{2,1,0:T(8,128)(2,1)}, bf16[8,2592,128]{2,1,0:T(8,128)(2,1)}, u32[]{:S(2)}, u32[]{:S(2)}) collective-permute-start(bf16[8,2592,128]{2,1,0:T(8,128)(2,1)} %get-tuple-element.133), channel_id=1, source_target_pairs={{0,1},{1,0},{2,3},{3,2},{4,5},{5,4},{6,7},{7,6},{8,9},{9,8},{10,11... | collective-permute-start | bytes 15925256 | tf_op jit(solution)/shard_map/ppermute | solution.py:765
  104.1 15.6 %all-to-all-start.2 = ((bf16[4,128,768]{2,1,0:T(8,128)(2,1)}), bf16[4,128,768]{2,1,0:T(8,128)(2,1)S(1)}, u32[]{:S(2)}, u32[]{:S(2)}) async-start(bf16[4,128,768]{2,1,0:T(8,128)(2,1)} %bitcast.36), calls=%async_computation.2 | async-start | bytes 1572864 | tf_op jit(solution)/shard_map/all_to_all | solution.py:1161
  119.7 7.7 %copy-start.4 = (bf16[4,128,768]{2,1,0:T(8,128)(2,1)}, bf16[4,128,768]{2,1,0:T(8,128)(2,1)S(1)}, u32[]{:S(2)}) copy-start(bf16[4,128,768]{2,1,0:T(8,128)(2,1)S(1)} %all-to-all-done.2) | copy-start | bytes 2359300
  127.4 59.6 %collective-permute-start.5 = (bf16[4,1296,128]{2,1,0:T(8,128)(2,1)}, bf16[4,1296,128]{2,1,0:T(8,128)(2,1)S(1)}, u32[]{:S(2)}, u32[]{:S(2)}) collective-permute-start(bf16[4,1296,128]{2,1,0:T(8,128)(2,1)} %get-tuple-element.158), channel_id=1, source_target_pairs={{0,2},{1,3},{2,0},{3,1},{4,6},{5,7},{6,4},{7,5},{8,10},{9,11},{10,... | collective-permute-start | bytes 3981320 | tf_op jit(solution)/shard_map/ppermute | solution.py:1101
  127.8 59.2 %collective-permute-start.6 = (bf16[4,1296,128]{2,1,0:T(8,128)(2,1)}, bf16[4,1296,128]{2,1,0:T(8,128)(2,1)S(1)}, u32[]{:S(2)}, u32[]{:S(2)}) collective-permute-start(bf16[4,1296,128]{2,1,0:T(8,128)(2,1)} %get-tuple-element.159), channel_id=1, source_target_pairs={{0,4},{1,5},{2,6},{3,7},{4,0},{5,1},{6,2},{7,3},{8,12},{9,13},{10,... | collective-permute-start | bytes 3981320 | tf_op jit(solution)/shard_map/ppermute | solution.py:1101
  129.7 58.5 %collective-permute-start.7 = (bf16[4,1296,128]{2,1,0:T(8,128)(2,1)}, bf16[4,1296,128]{2,1,0:T(8,128)(2,1)}, u32[]{:S(2)}, u32[]{:S(2)}) collective-permute-start(bf16[4,1296,128]{2,1,0:T(8,128)(2,1)} %get-tuple-element.160), channel_id=1, source_target_pairs={{0,6},{1,7},{2,4},{3,5},{4,2},{5,3},{6,0},{7,1},{8,14},{9,15},{10,... | collective-permute-start | bytes 3981320 | tf_op jit(solution)/shard_map/ppermute | solution.py:1101
  183.0 15.1 %all-to-all-start.3 = ((bf16[4,128,768]{2,1,0:T(8,128)(2,1)}), bf16[4,128,768]{2,1,0:T(8,128)(2,1)S(1)}, u32[]{:S(2)}, u32[]{:S(2)}) async-start(bf16[4,128,768]{2,1,0:T(8,128)(2,1)} %bitcast.35), calls=%async_computation.3 | async-start | bytes 1572864 | tf_op jit(solution)/shard_map/all_to_all | solution.py:1161
  186.5 6.2 %collective-permute-start.4 = (bf16[8,1504,128]{2,1,0:T(8,128)(2,1)}, bf16[8,1504,128]{2,1,0:T(8,128)(2,1)}, u32[]{:S(2)}, u32[]{:S(2)}) collective-permute-start(bf16[8,1504,128]{2,1,0:T(8,128)(2,1)} %get-tuple-element.157), channel_id=1, source_target_pairs={{0,1},{1,0},{2,3},{3,2},{4,5},{5,4},{6,7},{7,6},{8,9},{9,8},{10,11... | collective-permute-start | bytes 9240584 | tf_op jit(solution)/shard_map/ppermute | solution.py:765
  187.0 1.2 copy-start.14
  187.0 1.5 copy-start.15
  198.1 7.4 %copy-start.17 = (bf16[4,752,128]{2,1,0:T(8,128)(2,1)S(1)}, bf16[4,752,128]{2,1,0:T(8,128)(2,1)}, u32[]{:S(2)}) copy-start(bf16[4,752,128]{2,1,0:T(8,128)(2,1)} %get-tuple-element.179) | copy-start | bytes 2310148
  198.1 9.0 %copy-start.16 = (bf16[4,752,128]{2,1,0:T(8,128)(2,1)S(1)}, bf16[4,752,128]{2,1,0:T(8,128)(2,1)}, u32[]{:S(2)}) copy-start(bf16[4,752,128]{2,1,0:T(8,128)(2,1)} %get-tuple-element.180) | copy-start | bytes 2310148
  198.1 27.7 %copy-start.6 = (bf16[4,128,768]{2,1,0:T(8,128)(2,1)}, bf16[4,128,768]{2,1,0:T(8,128)(2,1)S(1)}, u32[]{:S(2)}) copy-start(bf16[4,128,768]{2,1,0:T(8,128)(2,1)S(1)} %all-to-all-done.3) | copy-start | bytes 2359300
  198.1 46.7 %all-to-all-start.4 = ((bf16[4,1296,128]{2,1,0:T(8,128)(2,1)}), bf16[4,1296,128]{2,1,0:T(8,128)(2,1)}, u32[]{:S(2)}, u32[]{:S(2)}) async-start(bf16[4,1296,128]{2,1,0:T(8,128)(2,1)} %feed_weights_two.1), calls=%async_computation.4 | async-start | bytes 2654208 | tf_op jit(solution)/shard_map/all_to_all | solution.py:1136
  203.8 23.7 %collective-permute-start.10 = (bf16[4,752,128]{2,1,0:T(8,128)(2,1)}, bf16[4,752,128]{2,1,0:T(8,128)(2,1)}, u32[]{:S(2)}, u32[]{:S(2)}) collective-permute-start(bf16[4,752,128]{2,1,0:T(8,128)(2,1)} %get-tuple-element.178), channel_id=1, source_target_pairs={{0,2},{1,3},{2,0},{3,1},{4,6},{5,7},{6,4},{7,5},{8,10},{9,11},{10,... | collective-permute-start | bytes 2310152 | tf_op jit(solution)/shard_map/ppermute | solution.py:1101
  205.5 34.8 %collective-permute-start.11 = (bf16[4,752,128]{2,1,0:T(8,128)(2,1)S(1)}, bf16[4,752,128]{2,1,0:T(8,128)(2,1)}, u32[]{:S(2)}, u32[]{:S(2)}) collective-permute-start(bf16[4,752,128]{2,1,0:T(8,128)(2,1)S(1)} %copy-done.17), channel_id=1, source_target_pairs={{0,4},{1,5},{2,6},{3,7},{4,0},{5,1},{6,2},{7,3},{8,12},{9,13},{10,... | collective-permute-start | bytes 2310152 | tf_op jit(solution)/shard_map/ppermute | solution.py:1101
  207.0 34.7 %collective-permute-start.12 = (bf16[4,752,128]{2,1,0:T(8,128)(2,1)S(1)}, bf16[4,752,128]{2,1,0:T(8,128)(2,1)}, u32[]{:S(2)}, u32[]{:S(2)}) collective-permute-start(bf16[4,752,128]{2,1,0:T(8,128)(2,1)S(1)} %copy-done.16), channel_id=1, source_target_pairs={{0,6},{1,7},{2,4},{3,5},{4,2},{5,3},{6,0},{7,1},{8,14},{9,15},{10,... | collective-permute-start | bytes 2310152 | tf_op jit(solution)/shard_map/ppermute | solution.py:1101
  225.8 51.4 %collective-permute-start.8 = (bf16[1024,768]{1,0:T(8,128)(2,1)}, bf16[1024,768]{1,0:T(8,128)(2,1)S(1)}, u32[]{:S(2)}, u32[]{:S(2)}) collective-permute-start(bf16[1024,768]{1,0:T(8,128)(2,1)} %get-tuple-element.175), channel_id=1, source_target_pairs={{0,2},{1,3},{2,0},{3,1},{4,6},{5,7},{6,4},{7,5},{8,10},{9,11},{10,... | collective-permute-start | bytes 4718600 | tf_op jit(solution)/shard_map/ppermute | solution.py:765
  227.5 22.4 %collective-permute-start.9 = (bf16[8,576,128]{2,1,0:T(8,128)(2,1)}, bf16[8,576,128]{2,1,0:T(8,128)(2,1)}, u32[]{:S(2)}, u32[]{:S(2)}) collective-permute-start(bf16[8,576,128]{2,1,0:T(8,128)(2,1)} %get-tuple-element.177), channel_id=1, source_target_pairs={{0,1},{1,0},{2,3},{3,2},{4,5},{5,4},{6,7},{7,6},{8,9},{9,8},{10,11... | collective-permute-start | bytes 3538952 | tf_op jit(solution)/shard_map/ppermute | solution.py:765
  244.8 34.0 %all-to-all-start.5 = ((bf16[4,752,128]{2,1,0:T(8,128)(2,1)}), bf16[4,752,128]{2,1,0:T(8,128)(2,1)}, u32[]{:S(2)}, u32[]{:S(2)}) async-start(bf16[4,752,128]{2,1,0:T(8,128)(2,1)} %self_weights_two.1), calls=%async_computation.5 | async-start | bytes 1540096 | tf_op jit(solution)/shard_map/all_to_all | solution.py:1136
  250.0 7.1 %copy-start.7 = (bf16[4,128,768]{2,1,0:T(8,128)(2,1)S(1)}, bf16[4,128,768]{2,1,0:T(8,128)(2,1)}, u32[]{:S(2)}) copy-start(bf16[4,128,768]{2,1,0:T(8,128)(2,1)} %copy-done.6) | copy-start | bytes 2359300
  253.6 17.1 %collective-permute-start.13 = (bf16[2,576,128]{2,1,0:T(8,128)(2,1)}, bf16[2,576,128]{2,1,0:T(8,128)(2,1)S(1)}, u32[]{:S(2)}, u32[]{:S(2)}) collective-permute-start(bf16[2,576,128]{2,1,0:T(8,128)(2,1)} %get-tuple-element.188), channel_id=1, source_target_pairs={{0,8},{1,9},{2,10},{3,11},{4,12},{5,13},{6,14},{7,15},{8,0},{9,1},... | collective-permute-start | bytes 884744 | tf_op jit(solution)/shard_map/ppermute | solution.py:1101
  255.6 15.1 %collective-permute-start.14 = (bf16[2,576,128]{2,1,0:T(8,128)(2,1)}, bf16[2,576,128]{2,1,0:T(8,128)(2,1)}, u32[]{:S(2)}, u32[]{:S(2)}) collective-permute-start(bf16[2,576,128]{2,1,0:T(8,128)(2,1)} %get-tuple-element.189), channel_id=1, source_target_pairs={{0,4},{1,5},{2,6},{3,7},{4,0},{5,1},{6,2},{7,3},{8,12},{9,13},{10,... | collective-permute-start | bytes 884744 | tf_op jit(solution)/shard_map/ppermute | solution.py:1101
  256.1 18.9 %collective-permute-start.15 = (bf16[2,576,128]{2,1,0:T(8,128)(2,1)}, bf16[2,576,128]{2,1,0:T(8,128)(2,1)}, u32[]{:S(2)}, u32[]{:S(2)}) collective-permute-start(bf16[2,576,128]{2,1,0:T(8,128)(2,1)} %get-tuple-element.190), channel_id=1, source_target_pairs={{0,12},{1,13},{2,14},{3,15},{4,8},{5,9},{6,10},{7,11},{8,4},{9,5},... | collective-permute-start | bytes 884744 | tf_op jit(solution)/shard_map/ppermute | solution.py:1101
  258.4 18.8 %copy-start = (bf16[1024,768]{1,0:T(8,128)(2,1)S(1)}, bf16[1024,768]{1,0:T(8,128)(2,1)}, u32[]{:S(2)}) copy-start(bf16[1024,768]{1,0:T(8,128)(2,1)} %get-tuple-element.200.refs_0_) | copy-start | bytes 4718596
  270.7 4.4 %copy-start.10 = (bf16[2,576,128]{2,1,0:T(8,128)(2,1)}, bf16[2,576,128]{2,1,0:T(8,128)(2,1)S(1)}, u32[]{:S(2)}) copy-start(bf16[2,576,128]{2,1,0:T(8,128)(2,1)S(1)} %collective-permute-done.13.refs_1_) | copy-start | bytes 884740
  277.2 1.4 copy-start.1
  278.2 8.9 %collective-permute-start.16 = (bf16[512,768]{1,0:T(8,128)(2,1)}, bf16[512,768]{1,0:T(8,128)(2,1)S(1)}, u32[]{:S(2)}, u32[]{:S(2)}) collective-permute-start(bf16[512,768]{1,0:T(8,128)(2,1)} %slice.22), channel_id=1, source_target_pairs={{0,1},{1,0},{2,3},{3,2},{4,5},{5,4},{6,7},{7,6},{8,9},{9,8},{10,11... | collective-permute-start | bytes 2359304 | tf_op jit(solution)/shard_map/ppermute | solution.py:765
  278.6 8.5 %collective-permute-start.17 = (bf16[512,768]{1,0:T(8,128)(2,1)S(1)}, bf16[512,768]{1,0:T(8,128)(2,1)}, u32[]{:S(2)}, u32[]{:S(2)}) collective-permute-start(bf16[512,768]{1,0:T(8,128)(2,1)S(1)} %slice.23), channel_id=1, source_target_pairs={{0,1},{1,0},{2,3},{3,2},{4,5},{5,4},{6,7},{7,6},{8,9},{9,8},{10,11... | collective-permute-start | bytes 2359304 | tf_op jit(solution)/shard_map/ppermute | solution.py:765
  278.8 14.9 %all-to-all-start.6 = ((bf16[4,288,128]{2,1,0:T(8,128)(2,1)}), bf16[4,288,128]{2,1,0:T(8,128)(2,1)S(1)}, u32[]{:S(2)}, u32[]{:S(2)}) async-start(bf16[4,288,128]{2,1,0:T(8,128)(2,1)} %cross_weights_two.1), calls=%async_computation.6 | async-start | bytes 589824 | tf_op jit(solution)/shard_map/all_to_all | solution.py:1136
  287.1 0.9 copy-start.9
  288.0 8.1 %copy-start.5 = (bf16[4,128,768]{2,1,0:T(8,128)(2,1)S(1)}, bf16[4,128,768]{2,1,0:T(8,128)(2,1)}, u32[]{:S(2)}) copy-start(bf16[4,128,768]{2,1,0:T(8,128)(2,1)} %copy-done.4) | copy-start | bytes 2359300
  293.7 0.7 copy-start.8
